TPU v7x, 32 devices: a whole 2x2x4 slice. The times are simulated.
32 devices in a mesh: groups: 2 (over y), lon: 4 (over z), lat: 2 (over x), sub: 2 (over core).
Axes of the slice: x: 2, y: 2, z: 4, core: 2. Of those that a mesh axis runs over, the one named last changes fastest.
Arguments:
- tokens: bfloat16 [512, 200, 384], P(('groups', 'lat', 'lon')), parts along dimension 0, may hold values from -130 to 130, as said below
- land_bits: int32 [512, 200], P(('groups', 'lat', 'lon')), parts along dimension 0, may hold values from 0 to 1, as said below
- ocean_list: int32 [4, 128], P(('groups', 'lat')), parts along dimension 0, may hold values from 0 to 128, as said below
- w_qkv: bfloat16 [2, 3, 384, 384], P(None, None, None, 'sub'), as said below
- w_out: bfloat16 [2, 384, 384], P(None, 'sub'), may hold values from -0.3125 to 0.3125
Outputs:
- advanced: bfloat16 [512, 200, 384], P(('groups', 'lat', 'lon')), parts along dimension 0
There are 2 independent parts, one for each index of `groups`. A program takes and returns all parts, laid end to end along the dimension named above; an argument that names none is the same for every part. Nothing has to cross between parts.
Inputs may be any that keep to these rules, and one draw needn't show every extreme that they name: `ocean_list`: each row lists its band's ocean windows in increasing order and then holds 128. A row lists at least 72 and at most 96 windows; some row lists exactly 96. In each window row of a band the listed windows form one run along longitude, which may wrap around. `land_bits`: every token of a window that its band's row of ocean_list does not list is land; in listed windows about a quarter of the tokens are land. `tokens`: finite values. `w_qkv`: entries lie within 165 / sqrt(384) in magnitude.
All inputs are finite; a program needn't handle non-finite values.
Results may differ from a plain program's by a relative error of at most 0.013.
Values may be sent and summed in bfloat16 or wider, within the bound.
No kernel may reach another device: no remote copies, remote signals or barrier semaphores. Data moves between devices by JAX's collectives and lax.ppermute only.
A program may use at most 64 MiB of HBM per device.

v0:
```python
import functools

import jax
import jax.numpy as jnp
import numpy as np
from jax import lax
from jax.experimental import pallas as pl
from jax.experimental.pallas import tpu as pltpu
from jax.sharding import PartitionSpec as P


HD = 32
WH = 10
WW = 20
T = WH * WW
ROWS = 4
TP = 208
KP = 256
LIMIT = 60
REC = 224
HALF = 112
SENT = HALF + 16
NEG = -1e30
SCALE = HD**-0.5 * 1.4426950408889634
f32 = jnp.float32
bf16 = jnp.bfloat16
NT = (((1,), (1,)), ((), ()))
HBM = pl.BlockSpec(memory_space=pltpu.HBM)
ANY = pl.BlockSpec(memory_space=pl.ANY)
VMEM = pl.BlockSpec(memory_space=pltpu.VMEM)


def normed(x):
    centred = x - jnp.mean(x, axis=-1, keepdims=True)
    variance = jnp.mean(centred * centred, axis=-1, keepdims=True)
    return (centred * lax.rsqrt(variance + 1e-05)).astype(bf16)


def blocks(pairs, load, again, land_rows, keeps, put, ready, weights, slots, nearly=None, heads=4, ahead=1):
    wqk, wv, wout = weights
    d = wv.shape[0]
    lane = lax.broadcasted_iota(jnp.int32, (1, 128), 1)
    masks = [jnp.where((lane >= HD * j) & (lane < HD * j + HD), 1.0, 0.0).astype(bf16) for j in range(4)]
    unit = jnp.broadcast_to(jnp.where(lane == 0, 1.0, 0.0), (TP, 128)).astype(bf16)
    ones = jnp.ones((16, TP), bf16)
    total = len(pairs)

    def before(t):
        norm, qk, values, _, _, bias, land = slots[t % 2]

        def normal(i):
            norm[i * TP : i * TP + T, :] = normed(load(t, i))

        def mask():
            rows = land_rows(t)
            land[...] = jnp.transpose(jnp.concatenate(rows + [rows[0]] * 6, axis=0))
            for i in range(2):
                bias[i] = jnp.where(lane == 0, land[:TP, i : i + 1] * NEG, 0.0).astype(bf16)

        def project(at):
            wide = lax.broadcasted_iota(jnp.int32, (1, 256), 1) + at
            got = lax.dot_general(norm[...], wqk[at : at + 256], NT, preferred_element_type=f32)
            qk[:, at : at + 256] = (got * jnp.where(wide < d, SCALE, 1.0)).astype(bf16)

        def value(i):
            got = lax.dot_general(wv[...], norm[i * TP : i * TP + TP], NT, preferred_element_type=f32)
            values[i] = got.astype(bf16)

        return (
            [functools.partial(normal, i) for i in range(2)] + [mask]
            + [functools.partial(project, at) for at in range(0, 2 * d, 256)]
            + [functools.partial(value, i) for i in range(2)]
        )

    def after(t):
        _, _, _, mixed, joined, _, land = slots[t % 2]
        held = {}

        def turn(i):
            joined[i * TP : i * TP + TP] = jnp.transpose(mixed[i])

        def out():
            held["update"] = jnp.dot(joined[...], wout[...], preferred_element_type=f32)

        def add(i):
            keep = (1.0 - land[:T, i : i + 1]) * keeps(t, i)
            put(t, i, (again(t, i) + held["update"][i * TP : i * TP + T] * keep).astype(bf16))

        return [functools.partial(turn, i) for i in range(2)] + [out] + [functools.partial(add, i) for i in range(2)]

    units = [
        (t, i, g, tuple(range(a, a + heads)))
        for t in range(total) for i in range(2) for g in range(d // 128) for a in range(0, 4, heads)
    ]
    per = len(units) // total
    scores, probs = {}, {}

    def score(u):
        t, i, g, hs = units[u]
        qk, bias = slots[t % 2][1], slots[t % 2][5]
        k = qk[i * TP : i * TP + TP, d + 128 * g : d + 128 * g + 128]
        q = jnp.concatenate([qk[i * TP : i * TP + TP, 128 * g : 128 * g + 128], unit], axis=1)
        b = bias[i]
        keyed = jnp.concatenate([jnp.concatenate([k * masks[j], b], axis=1) for j in hs], axis=0)
        got = lax.dot_general(keyed, q, NT, preferred_element_type=f32)
        scores[u] = [got[n * TP : n * TP + TP] for n in range(len(hs))]

    def soften(u):
        probs[u] = [
            jnp.exp2((s - jnp.max(s, axis=0, keepdims=True)).astype(bf16)) for s in scores.pop(u)
        ]

    def mix(u):
        t, i, g, hs = units[u]
        values, mixed = slots[t % 2][2], slots[t % 2][3]
        for j, p in zip(hs, probs.pop(u)):
            at = 128 * g + HD * j
            both = jnp.dot(
                jnp.concatenate([values[i, at : at + HD], ones], axis=0), p, preferred_element_type=f32
            )
            mixed[i, at : at + HD] = (both[:HD] * (1.0 / both[HD : HD + 1])).astype(bf16)

    for piece in before(0):
        piece()
    ready()
    pieces, step, place = [], 1.0, 1
    for k in range(len(units) + 2 * ahead):
        t, at = k // per, k % per
        if at == 2 * ahead:
            pieces = (after(t - 1) if t else []) + (before(t + 1) if t + 1 < total else [])
            step, place = (per - 2 * ahead) / (len(pieces) + 1), 1
        if k < len(units):
            score(k)
        if 0 <= k - ahead < len(units):
            soften(k - ahead)
        if 0 <= k - 2 * ahead:
            mix(k - 2 * ahead)
        while pieces and (at == per - 1 or at - 2 * ahead + 1 >= place * step):
            pieces.pop(0)()
            place += 1
    if nearly is not None:
        nearly(total - 1)
    for piece in pieces + after(total - 1):
        piece()


def paired(windows):
    padded = list(windows) + [windows[-1]] * (len(windows) % 2)
    return [padded[n : n + 2] for n in range(0, len(padded), 2)]


def weight_copies(block, own_qkv, own_out, other_qkv, other_out, weights, sem):
    wqk, wv, wout = weights
    half = own_out.shape[1]
    pairs = []
    for n, (qkv, out) in enumerate(((own_qkv, own_out), (other_qkv, other_out))):
        for part in range(2):
            pairs.append((qkv.at[block, part], wqk.at[pl.ds((2 * part + n) * half, half)]))
        pairs.append((qkv.at[block, 2], wv.at[pl.ds(n * half, half)]))
        pairs.append((out.at[block], wout.at[pl.ds(n * half, half)]))
    return [pltpu.make_async_copy(a, b, sem.at[n]) for n, (a, b) in enumerate(pairs)]


def clear_pads(slots):
    for slot in slots:
        for i in range(2):
            slot[0][i * TP + TP - 16 : i * TP + TP, :] = jnp.zeros((16, slot[0].shape[1]), bf16)


LOW = T - HALF + 8
MID = T // 2 // 16 * 16


def side_masks(left):
    token = lax.broadcasted_iota(jnp.int32, left.shape, 0)
    left[...] = jnp.where(token % WW < WW // 2, 1.0, 0.0).astype(bf16)


def merged(at, left, d):
    def pick(below, lo, hi):
        side = jnp.concatenate([left[lo:hi]] * (d // 128), axis=1) > 0.5
        return jnp.where(side, at(1, below, slice(lo, hi)), at(0, below, slice(lo, hi)))

    row = lax.broadcasted_iota(jnp.int32, (HALF - MID, d), 0) + MID
    middle = jnp.where(row < T // 2, pick(1, MID, HALF).astype(f32), pick(0, MID, HALF).astype(f32)).astype(bf16)
    return jnp.concatenate([pick(1, 0, MID), middle, pick(0, HALF, T)], axis=0)


class Plan:
    def __init__(self, columns):
        self.c = c = columns
        self.low = low = (c + 1) // 2
        self.up = c > low
        last = ROWS - 1
        sent = [(0, r) for r in range(ROWS)]
        sent += [(x, 0) for x in range(1, min(low, c - 1) + 1)]
        sent += [(x, last) for x in range(max(low, 1), c)]
        self.first_a = sent
        self.first_b = [(x, r) for x in range(c) for r in range(ROWS) if (x, r) not in sent]
        self.to_left = [(0, r) for r in range(ROWS)]
        self.to_above = [(x, 0) for x in range(min(low, c - 1) + 1)]
        self.to_below = [(x, last) for x in range(low, c)]
        self.to_diag = (0, last) if self.up else (0, 0)
        self.rim = [(c - 1, r) for r in range(last)]
        self.lower = [(x, last) for x in range(low)]
        self.upper = [(x, -1) for x in range(low, c)]
        self.inner = [(x, r) for x in range(c - 1) for r in range(last)]
        self.extra = len(self.rim) % 2 if self.inner else 0
        self.some = self.rim + self.inner[: self.extra]
        self.rest = self.inner[self.extra :]
        self.back_right = [(c - 1, r) for r in (range(-1, last) if self.up else range(ROWS))]

    def index(self, window):
        return window[0] * ROWS + window[1]


def first_kernel(plan, which, *refs):
    windows = plan.first_b if which else plan.first_a
    tokens, land, ocean = refs[:3]
    sources, refs = refs[3:7], refs[7:]
    if which:
        refs = refs[1:]
    out, refs = refs[0], refs[1:]
    if which == 0:
        left, above, below, diag = refs[:4]
        refs = refs[4:]
    x_in, rec, bits, sem_in, sem_out, sem_w = refs[:6]
    weights, slots = refs[6:9], (refs[9:16], refs[16:23])
    pairs = paired(list(range(len(windows))))
    start = lax.axis_index("sub") * (plan.c * ROWS)
    copies = weight_copies(0, *sources, weights, sem_w)
    reads = [
        pltpu.make_async_copy(tokens.at[start + plan.index(w)], x_in.at[j], sem_in.at[j])
        for j, w in enumerate(windows)
    ]
    for copy in reads[:2] + copies + reads[2:]:
        copy.start()
    clear_pads(slots)
    bits[...] = jnp.ones(bits.shape, f32)
    bits[:, :T] = land[...].astype(f32)
    for copy in reads[:2] + copies:
        copy.wait()

    def ready():
        for copy in reads[2:]:
            copy.wait()

    def row(j):
        return bits[pl.ds(start + plan.index(windows[j]), 1), :]

    def listed(j):
        ident = lax.axis_index("lon") * (plan.c * ROWS * lax.axis_size("sub")) + start + plan.index(windows[j])
        return jnp.max(jnp.where(ocean[...] == ident, 1.0, 0.0), axis=1, keepdims=True)

    def put(t, i, value):
        rec[pairs[t][i], :T, :] = value

    def load(t, i):
        return x_in[pairs[t][i]].astype(f32)

    ends = [[(rec.at[j], out.at[plan.index(w)])] for j, w in enumerate(windows)]
    if which == 0:
        slot = {w: j for j, w in enumerate(windows)}
        for k, w in enumerate(plan.to_left):
            ends[slot[w]].append((rec.at[slot[w]], left.at[k]))
        halves = [(above, k, w, 0) for k, w in enumerate(plan.to_above)]
        halves += [(below, k, w, LOW) for k, w in enumerate(plan.to_below)]
        halves += [(diag, 0, plan.to_diag, LOW if plan.up else 0)]
        for to, k, w, at in halves:
            j = slot[w]
            ends[j].append((rec.at[j, pl.ds(at, HALF)], to.at[k, pl.ds(0, HALF)]))
            ends[j].append((rec.at[j, pl.ds(TP, REC - TP)], to.at[k, pl.ds(HALF, SENT - HALF)]))
    numbers = iter(range(len(windows) + 40))
    ends = [[pltpu.make_async_copy(a, b, sem_out.at[next(numbers)]) for a, b in group] for group in ends]

    def send(lo, hi):
        for j in range(lo, hi):
            for copy in ends[j]:
                copy.start()

    for j in range(len(windows)):
        rec[j, TP:, :KP] = jnp.broadcast_to(row(j).astype(bf16), (REC - TP, KP))
    blocks(
        pairs, load, load, lambda t: [row(j) for j in pairs[t]], lambda t, i: listed(pairs[t][i]), put, ready,
        weights, slots, lambda t: send(0, 2 * t),
    )
    send(2 * (len(pairs) - 1), len(windows))
    for copy in (c for group in ends for c in group):
        copy.wait()


def second_kernel(plan, which, d, *refs):
    first, sources, refs = refs[0], refs[1:5], refs[5 + which :]
    if which == 0:
        right, above, below, diag = refs[:4]
        refs = refs[4:]
    out, refs = refs[0], refs[1:]
    if which == 0:
        to_right, to_below, to_above, to_diag = refs[:4]
        refs = refs[4:]
    ext, res, kept, left, sem_in, sem_out, sem_w = refs[:7]
    weights, slots = refs[7:10], (refs[10:17], refs[17:24])
    side_masks(left)
    c = plan.c
    windows = plan.rest if which else plan.some
    all_windows = list(windows) if which else windows + plan.lower + plan.upper
    copies, asked = [], set()
    for x, r in all_windows:
        for place in ((x, r), (x + 1, r), (x, r + 1), (x + 1, r + 1)):
            if place in asked:
                continue
            asked.add(place)
            u, v = place
            if 0 <= v < ROWS:
                copies.append((first.at[plan.index(place)] if u < c else right.at[v], ext.at[u, v + 1]))
                continue
            if v == ROWS:
                source, at = above.at[u] if u < len(plan.to_above) else diag.at[0], 0
            else:
                source, at = below.at[u - plan.low] if u < c else diag.at[0], LOW
            copies.append((source.at[pl.ds(0, HALF)], ext.at[u, v + 1, pl.ds(at, HALF)]))
            copies.append((source.at[pl.ds(HALF, SENT - HALF)], ext.at[u, v + 1, pl.ds(TP, REC - TP)]))
    reads = [pltpu.make_async_copy(a, b, sem_in.at[n]) for n, (a, b) in enumerate(copies)]
    loads = weight_copies(1, *sources, weights, sem_w)
    early = 6 if len(reads) > 6 else len(reads)
    for copy in reads[:early] + loads + reads[early:]:
        copy.start()
    clear_pads(slots)
    token = lax.broadcasted_iota(jnp.int32, (1, KP), 1)
    left_row, top_row = token % WW < WW // 2, token < T // 2
    for copy in reads[:early] + loads:
        copy.wait()

    def ready():
        for copy in reads[early:]:
            copy.wait()

    def gathered(x, r):
        return merged(lambda i, j, rows: ext[x + i, r + 1 + j, rows, :], left, d)

    def land_of(x, r):
        a, b, e, f = [
            ext[x + i, r + 1 + j, TP : TP + 16, :KP].astype(f32)[:1] for j in (0, 1) for i in (0, 1)
        ]
        return jnp.where(
            token < T, jnp.where(top_row, jnp.where(left_row, f, e), jnp.where(left_row, b, a)), 1.0
        )

    places = [(w[0], w[1], n, 1.0) for n, w in enumerate(windows)]
    base = len(windows)

    def moving(lower_set, on):
        found = []
        for j in range(len(plan.lower)):
            other = min(j, max(len(plan.upper) - 1, 0))
            x = jnp.where(lower_set, j, plan.low + other)
            r = jnp.where(lower_set, ROWS - 1, -1)
            found.append((x, r, base + jnp.where(lower_set, j, len(plan.lower) + other), on))
        return found

    ends = [(res.at[j], out.at[j]) for j in range(len(all_windows))]
    if which == 0:
        slot = {w: j for j, w in enumerate(all_windows)}
        ends += [(res.at[slot[w]], to_right.at[k]) for k, w in enumerate(plan.back_right)]
        ends += [(res.at[slot[w], pl.ds(0, HALF)], to_below.at[k]) for k, w in enumerate(plan.lower)]
        tail = pl.ds(LOW, T - LOW)
        ends += [(res.at[slot[w], tail], to_above.at[k]) for k, w in enumerate(plan.upper)]
        corner = plan.back_right[0] if plan.up else plan.back_right[-1]
        ends += [(res.at[slot[corner], tail if plan.up else pl.ds(0, HALF)], to_diag.at[0])]
    ends = [pltpu.make_async_copy(a, b, sem_out.at[n]) for n, (a, b) in enumerate(ends)]
    band, bands = lax.axis_index("lat"), lax.axis_size("lat")
    listing = [paired(places)] if places else [[]]
    if which == 0:
        lower_set = band < bands - 1 if plan.up else band >= 0
        on = jnp.where(lower_set, band < bands - 1, band > 0).astype(f32)
        listing[0] = listing[0] + paired(moving(lower_set, on))

    def nearly(t):
        for copy in ends[: 2 * t]:
            copy.start()

    def run(pairs, ready, nearly=None):
        def load(t, i):
            x, r, _, _ = pairs[t][i]
            value = gathered(x, r)
            kept[2 * (t % 3) + i] = value
            return value.astype(f32)

        def again(t, i):
            return kept[2 * (t % 3) + i].astype(f32)

        def put(t, i, value):
            res[pairs[t][i][2]] = value

        blocks(
            pairs, load, again, lambda t: [land_of(x, r) for x, r, _, _ in pairs[t]], lambda t, i: pairs[t][i][3],
            put, ready, weights, slots, nearly,
        )

    run(listing[0], ready, nearly if which else None)
    if which == 0 and plan.up:
        both = (band > 0) & (band < bands - 1)
        if bands > 2:

            @pl.when(both)
            def _():
                run(paired(moving(band < 0, jnp.float32(1))), lambda: None)

        for n, (w, idle) in enumerate(
            [(w, band == bands - 1) for w in plan.lower] + [(w, band == 0) for w in plan.upper]
        ):

            @pl.when(idle)
            def _(n=n, w=w):
                res[base + n] = gathered(*w)

    for copy in ends[2 * (len(listing[0]) - 1) if which else 0 :]:
        copy.start()
    for copy in ends:
        copy.wait()


def place_kernel(plan, which, d, *refs):
    raw_c, raw_d, lefts, aboves, belows, corner = refs[:6]
    out, grid, fin, left, sem_in, sem_out = refs[6 + which :]
    c = plan.c
    tail, head = pl.ds(LOW, T - LOW), pl.ds(0, HALF)
    moves = {}
    for j, (x, r) in enumerate(plan.some + plan.lower + plan.upper):
        moves[x, r] = (raw_c.at[j], grid.at[x + 1, r + 1])
    for j, (x, r) in enumerate(plan.rest):
        moves[x, r] = (raw_d.at[j], grid.at[x + 1, r + 1])
    for k, (_, r) in enumerate(plan.back_right):
        moves[-1, r] = (lefts.at[k], grid.at[0, r + 1])
    for k, (x, _) in enumerate(plan.lower):
        moves[x, -1] = (aboves.at[k], grid.at[x + 1, 0, head])
    for k, (x, _) in enumerate(plan.upper):
        moves[x, ROWS - 1] = (belows.at[k], grid.at[x + 1, ROWS, tail])
    if plan.up:
        moves[-1, ROWS - 1] = (corner.at[0], grid.at[0, ROWS, tail])
    else:
        moves[-1, -1] = (corner.at[0], grid.at[0, 0, head])
    copies = {k: pltpu.make_async_copy(*moves[k], sem_in.at[n]) for n, k in enumerate(sorted(moves))}
    for k in sorted(moves):
        copies[k].start()
    side_masks(left)
    me = lax.axis_index("sub")
    start = (1 - me if which else me) * (c * ROWS)
    for x in range(-1, c):
        for r in range(-1, ROWS):
            copies[x, r].wait()
        if x < 0:
            continue

        def body(r, _, x=x):
            w = x * ROWS + r
            fin[w] = merged(
                lambda i, j, rows: grid[x + 1 - i, r + 1 - j, rows, :], left, d
            )
            pltpu.make_async_copy(fin.at[w], out.at[start + w], sem_out.at[w]).start()
            return 0

        lax.fori_loop(0, ROWS, body, 0)
    for w in range(c * ROWS):
        pltpu.make_async_copy(fin.at[w], out.at[start + w], sem_out.at[w]).wait()


def ring(value, axes, by):
    sizes = [lax.axis_size(a) for a in axes]
    total = int(np.prod(sizes))
    grid = np.arange(total).reshape(sizes)
    moved = grid
    for dim, step in enumerate(by):
        moved = np.roll(moved, -step, axis=dim)
    pairs = list(zip(grid.ravel().tolist(), moved.ravel().tolist()))
    return lax.ppermute(value, tuple(axes), pairs)


def beside(value, lat, step):
    lon, sub, lats = lax.axis_size("lon"), lax.axis_size("sub"), lax.axis_size("lat")
    ident = np.arange(lon * lats * sub).reshape(lon, lats, sub)
    line = np.transpose(ident, (1, 0, 2)).reshape(lats, lon * sub)
    axes = ("lon", "lat", "sub")
    if not lat:
        line, axes = np.arange(lon * sub)[None], ("lon", "sub")
    moved = np.roll(line, (-lat, -step), axis=(0, 1))
    return lax.ppermute(value, axes, list(zip(line.ravel().tolist(), moved.ravel().tolist())))


def call(body, ins, outs, scratch, alias, flops, limit):
    total = sum(int(np.prod(o.shape)) * 2 for o in outs)
    return pl.pallas_call(
        body, in_specs=ins, out_specs=[ANY] * len(outs), out_shape=outs, scratch_shapes=scratch,
        input_output_aliases=alias,
        compiler_params=pltpu.CompilerParams(vmem_limit_bytes=limit * 2**20),
        cost_estimate=pl.CostEstimate(flops=flops, bytes_accessed=2 * total, transcendentals=0),
    )


def shards(tokens, land_bits, ocean_list, w_qkv, w_out):
    window_count, _, d = tokens.shape
    mine = window_count // lax.axis_size("sub")
    plan = Plan(mine // ROWS)
    turned = jnp.swapaxes(w_qkv, 2, 3)
    other_qkv, other_out = ring((turned, w_out), ("sub",), (1,))
    weights = (turned, w_out, other_qkv, other_out)
    per_window = 12_000_000_000

    def shape(*s):
        return jax.ShapeDtypeStruct(s, bf16)

    def sems(*counts):
        return [pltpu.SemaphoreType.DMA((n,)) for n in counts]

    slot = [
        pltpu.VMEM((2 * TP, d), bf16), pltpu.VMEM((2 * TP, 2 * d), bf16), pltpu.VMEM((2, d, TP), bf16),
        pltpu.VMEM((2, d, TP), bf16), pltpu.VMEM((2 * TP, d), bf16), pltpu.VMEM((2, TP, 128), bf16),
        pltpu.VMEM((KP, 8), f32),
    ]
    work = [pltpu.VMEM((2 * d, d), bf16), pltpu.VMEM((d, d), bf16), pltpu.VMEM((d, d), bf16)] + slot + slot

    def first_call(which, outs, extra, alias):
        n = len(plan.first_b if which else plan.first_a)
        scratch = [pltpu.VMEM((n, T, d), bf16), pltpu.VMEM((n, REC, d), bf16), pltpu.VMEM((window_count, KP), f32)]
        scratch += sems(n, n + 40, 8) + work
        specs = [HBM, VMEM, VMEM] + [ANY] * (4 + len(extra))
        return call(
            functools.partial(first_kernel, plan, which), specs, outs, scratch, alias,
            n * per_window, LIMIT,
        )(tokens, land_bits, ocean_list, *weights, *extra)

    halves = [shape(n, SENT, d) for n in (len(plan.to_above), max(len(plan.to_below), 1), 1)]
    first, left, above, below, diag = first_call(0, [shape(mine, REC, d), shape(ROWS, REC, d)] + halves, (), {})
    right = beside(left, 0, -1)
    from_below = ring(above, ("lat",), (-1,))
    from_above = ring(below, ("lat",), (1,)) if plan.up else below
    from_diag = beside(diag, 1 if plan.up else -1, -1)
    if plan.first_b:
        first = first_call(1, [shape(mine, REC, d)], (first,), {7: 0})[0]

    def second_call(which, ins, outs):
        n = outs[0].shape[0]
        scratch = [pltpu.VMEM((plan.c + 1, ROWS + 2, REC, d), bf16), pltpu.VMEM((n, T, d), bf16)]
        scratch += [pltpu.VMEM((6, T, d), bf16), pltpu.VMEM((T, 128), bf16)] + sems(80, n + 20, 8) + work
        return call(
            functools.partial(second_kernel, plan, which, d), [ANY] * len(ins), outs, scratch,
            {}, n * per_window, LIMIT,
        )(*ins)

    rim = len(plan.some) + len(plan.lower) + len(plan.upper)
    raw_c, to_right, to_below, to_above, to_diag = second_call(
        0,
        (first,) + weights + (right, from_below, from_above, from_diag),
        [
            shape(rim, T, d), shape(ROWS, T, d), shape(len(plan.lower), HALF, d),
            shape(max(len(plan.upper), 1), T - LOW, d), shape(1, T - LOW if plan.up else HALF, d),
        ],
    )
    lefts = beside(to_right, 0, 1)
    aboves = ring(to_below, ("lat",), (1,))
    belows = ring(to_above, ("lat",), (-1,)) if plan.up else to_above
    corner = beside(to_diag, -1 if plan.up else 1, 1)
    other_c = ring(raw_c, ("sub",), (1,))
    raw_d = second_call(1, (first,) + weights + (to_diag,), [shape(len(plan.rest), T, d)])[0] if plan.rest else raw_c
    other_d = ring(raw_d, ("sub",), (1,)) if plan.rest else other_c
    here = (lefts, aboves, belows, corner)
    there = ring(here, ("sub",), (1,))

    def place_call(which, *ins):
        return call(
            functools.partial(place_kernel, plan, which, d), [ANY] * 6 + [HBM] * which,
            [shape(window_count, T, d)],
            [pltpu.VMEM((plan.c + 1, ROWS + 1, T, d), bf16), pltpu.VMEM((mine, T, d), bf16), pltpu.VMEM((T, 128), bf16)] + sems(60, mine),
            {6: 0} if which else {}, 100_000_000, LIMIT,
        )(*ins)[0]

    out = place_call(0, raw_c, raw_d, *here)
    return place_call(1, other_c, other_d, *there, out)


def solution(mesh):
    placed = (
        P(("groups", "lat", "lon"), None, None),
        P(("groups", "lat", "lon"), None),
        P(("groups", "lat"), None),
        P(None, None, None, "sub"),
        P(None, "sub", None),
    )
    return jax.shard_map(
        shards,
        mesh=mesh,
        in_specs=placed,
        out_specs=P(("groups", "lat", "lon"), None, None),
        check_vma=False,
    )
```

profile of v0, /device:TPU:0, one launch (start us, length us, event | category | flops | bytes accessed | tf_op | source)
XLA Modules:
  0.0 94.4 jit_solution(13822102003281597873)
XLA Ops:
  0.5 2.7 %collective-permute-done.1.refs_6_.refs_4_ = bf16[2,192,384]{2,1,0:T(8,128)(2,1)S(1)} collective-permute-done((bf16[2,192,384]{2,1,0:T(8,128)(2,1)}, bf16[2,192,384]{2,1,0:T(8,128)(2,1)S(1)}, u32[]{:S(2)}, u32[]{:S(2)}) %collective-permute-start.1) | collective-permute-done | bytes 294944 | tf_op jit(solution)/shard_map/ppermute | solution.py:476
  3.2 0.7 copy-done.10
  3.9 0.9 copy-done.8
  4.8 13.6 %shard_map.55 = (bf16[16,224,384]{2,1,0:T(8,128)(2,1)}, bf16[4,224,384]{2,1,0:T(8,128)(2,1)}, bf16[3,128,384]{2,1,0:T(8,128)(2,1)}, bf16[2,128,384]{2,1,0:T(8,128)(2,1)}, bf16[1,128,384]{2,1,0:T(8,128)(2,1)}) custom-call(bf16[32,200,384]{2,1,0:T(8,128)(2,1)} %refs_0_.3, s32[32,200]{1,0:T(8,128)} %refs_1_.3, s32[1,128]{1,0:T(1,128)} %refs_2_.5, ...), custom_call_target="tpu_custom_call" | custom-call | flops 96000000000 | bytes 8060928 | tf_op jit(solution)/shard_map/pallas_call | solution.py:527
  18.4 5.7 %collective-permute-start.5 = (bf16[1,128,384]{2,1,0:T(8,128)(2,1)}, bf16[1,128,384]{2,1,0:T(8,128)(2,1)S(1)}, u32[]{:S(2)}, u32[]{:S(2)}) collective-permute-start(bf16[1,128,384]{2,1,0:T(8,128)(2,1)} %get-tuple-element.19), channel_id=1, source_target_pairs={{0,15},{1,2},{4,3},{5,6},{8,7},{9,10},{12,11},{13,14},{2,13},{3,0}... | collective-permute-start | bytes 294920 | tf_op jit(solution)/shard_map/ppermute | solution.py:487
  24.1 0.5 collective-permute-start.4
  24.6 1.5 %collective-permute-start.3 = (bf16[3,128,384]{2,1,0:T(8,128)(2,1)}, bf16[3,128,384]{2,1,0:T(8,128)(2,1)S(1)}, u32[]{:S(2)}, u32[]{:S(2)}) collective-permute-start(bf16[3,128,384]{2,1,0:T(8,128)(2,1)} %get-tuple-element.17), channel_id=1, source_target_pairs={{0,2},{2,0},{1,3},{3,1},{4,6},{6,4},{5,7},{7,5},{8,10},{10,8},{9,1... | collective-permute-start | bytes 884744 | tf_op jit(solution)/shard_map/ppermute | solution.py:476
  26.1 13.3 %shard_map.56.refs_0_ = bf16[16,224,384]{2,1,0:T(8,128)(2,1)} custom-call(bf16[32,200,384]{2,1,0:T(8,128)(2,1)} %refs_0_.3, s32[32,200]{1,0:T(8,128)} %refs_1_.3, s32[1,128]{1,0:T(1,128)} %refs_2_.5, bf16[2,3,192,384]{3,2,1,0:T(8,128)(2,1)} %bitcast.3, bf16[2,192,384]{2,1,0:T(8,128)(2,1)} %refs_2_.7, ...), custom_call_target="tpu_custom_call", output_to_operand_aliasing={{}: (7, {})} | custom-call | flops 96000000000 | bytes 5505024 | tf_op jit(solution)/shard_map/pallas_call | solution.py:527
  39.5 0.6 copy-done.14
  40.3 0.9 copy-done.9
  41.1 12.2 %shard_map.57 = (bf16[8,200,384]{2,1,0:T(8,128)(2,1)}, bf16[4,200,384]{2,1,0:T(8,128)(2,1)}, bf16[2,112,384]{2,1,0:T(8,128)(2,1)}, bf16[2,104,384]{2,1,0:T(8,128)(2,1)}, bf16[1,104,384]{2,1,0:T(8,128)(2,1)}) custom-call(bf16[16,224,384]{2,1,0:T(8,128)(2,1)} %shard_map.56.refs_0_, bf16[2,3,192,384]{3,2,1,0:T(8,128)(2,1)} %bitcast.4, ...), custom_call_target="tpu_custom_call" | custom-call | flops 96000000000 | bytes 4509696 | tf_op jit(solution)/shard_map/pallas_call | solution.py:545
  53.3 0.6 collective-permute-start.8
  53.9 13.4 %shard_map.58.refs_1_ = bf16[8,200,384]{2,1,0:T(8,128)(2,1)} custom-call(bf16[16,224,384]{2,1,0:T(8,128)(2,1)} %shard_map.56.refs_0_, bf16[2,3,192,384]{3,2,1,0:T(8,128)(2,1)} %bitcast.5, bf16[2,192,384]{2,1,0:T(8,128)(2,1)} %refs_2_.7, bf16[2,3,192,384]{3,2,1,0:T(8,128)(2,1)} %copy-done.8, bf16[2,192,384]{2,1,0:T(8,128)(2,1)} %copy-done.10, ...), custom_call_target="tpu_custom_call" | custom-call | flops 96000000000 | bytes 2457600 | tf_op jit(solution)/shard_map/pallas_call | solution.py:545
  67.9 0.5 collective-permute-start.14
  68.5 6.0 %collective-permute-done.14.refs_5_ = bf16[1,104,384]{2,1,0:T(8,128)(2,1)S(1)} collective-permute-done((bf16[1,104,384]{2,1,0:T(8,128)(2,1)S(1)}, bf16[1,104,384]{2,1,0:T(8,128)(2,1)S(1)}, u32[]{:S(2)}, u32[]{:S(2)}) %collective-permute-start.14) | collective-permute-done | bytes 79904 | tf_op jit(solution)/shard_map/ppermute | solution.py:487
  74.5 0.6 collective-permute-start.10
  75.1 0.7 collective-permute-done.15.refs_5_
  75.7 0.8 collective-permute-start.12
  76.6 5.2 %collective-permute-done.10.refs_3_ = bf16[2,112,384]{2,1,0:T(8,128)(2,1)S(1)} collective-permute-done((bf16[2,112,384]{2,1,0:T(8,128)(2,1)S(1)}, bf16[2,112,384]{2,1,0:T(8,128)(2,1)S(1)}, u32[]{:S(2)}, u32[]{:S(2)}) %collective-permute-start.10) | collective-permute-done | bytes 172064 | tf_op jit(solution)/shard_map/ppermute | solution.py:476
  81.8 3.0 %collective-permute-done.12.refs_4_ = bf16[2,104,384]{2,1,0:T(8,128)(2,1)} collective-permute-done((bf16[2,104,384]{2,1,0:T(8,128)(2,1)}, bf16[2,104,384]{2,1,0:T(8,128)(2,1)}, u32[]{:S(2)}, u32[]{:S(2)}) %collective-permute-start.12) | collective-permute-done | bytes 159776 | tf_op jit(solution)/shard_map/ppermute | solution.py:476
  84.8 3.5 %shard_map.59.refs_6_ = bf16[32,200,384]{2,1,0:T(8,128)(2,1)} custom-call(bf16[8,200,384]{2,1,0:T(8,128)(2,1)} %get-tuple-element.20.refs_0_, bf16[8,200,384]{2,1,0:T(8,128)(2,1)} %shard_map.58.refs_1_, bf16[4,200,384]{2,1,0:T(8,128)(2,1)} %copy-done.3, bf16[2,112,384]{2,1,0:T(8,128)(2,1)} %copy-done.5, ...), custom_call_target="tpu_custom_call" | custom-call | flops 100000000 | bytes 9830400 | tf_op jit(solution)/shard_map/pallas_call | solution.py:570
  88.4 0.6 copy-done.4
  89.7 1.0 %copy-done.1 = bf16[8,200,384]{2,1,0:T(8,128)(2,1)} copy-done((bf16[8,200,384]{2,1,0:T(8,128)(2,1)}, bf16[8,200,384]{2,1,0:T(8,128)(2,1)S(1)}, u32[]{:S(2)}) %copy-start.1) | copy-done | bytes 1228824
  90.7 3.5 %shard_map.60 = bf16[32,200,384]{2,1,0:T(8,128)(2,1)} custom-call(bf16[8,200,384]{2,1,0:T(8,128)(2,1)} %copy-done, bf16[8,200,384]{2,1,0:T(8,128)(2,1)} %copy-done.1, bf16[4,200,384]{2,1,0:T(8,128)(2,1)} %copy-done.2, bf16[2,112,384]{2,1,0:T(8,128)(2,1)} %copy-done.4, ...), custom_call_target="tpu_custom_call", output_to_operand_aliasing={{}: (6, {})} | custom-call | flops 100000000 | bytes 9830400 | tf_op jit(solution)/shard_map/pallas_call | solution.py:570
  (46 shorter events, 2.1 us)
Async XLA Ops:
  0.0 3.2 %collective-permute-start = (bf16[2,3,192,384]{3,2,1,0:T(8,128)(2,1)}, bf16[2,3,192,384]{3,2,1,0:T(8,128)(2,1)S(1)}, u32[]{:S(2)}, u32[]{:S(2)}) collective-permute-start(bf16[2,3,192,384]{3,2,1,0:T(8,128)(2,1)} %bitcast.1), channel_id=1, source_target_pairs={{0,1},{1,0},{2,3},{3,2},{4,5},{5,4},{6,7},{7,6},{8,9},{9,8},{10,11... | collective-permute-start | bytes 2654216 | tf_op jit(solution)/shard_map/ppermute | solution.py:476
  0.5 2.7 %collective-permute-start.1 = (bf16[2,192,384]{2,1,0:T(8,128)(2,1)}, bf16[2,192,384]{2,1,0:T(8,128)(2,1)S(1)}, u32[]{:S(2)}, u32[]{:S(2)}) collective-permute-start(bf16[2,192,384]{2,1,0:T(8,128)(2,1)} %refs_2_.7), channel_id=1, source_target_pairs={{0,1},{1,0},{2,3},{3,2},{4,5},{5,4},{6,7},{7,6},{8,9},{9,8},{10,11... | collective-permute-start | bytes 884744 | tf_op jit(solution)/shard_map/ppermute | solution.py:476
  18.4 21.0 %collective-permute-start.5 = (bf16[1,128,384]{2,1,0:T(8,128)(2,1)}, bf16[1,128,384]{2,1,0:T(8,128)(2,1)S(1)}, u32[]{:S(2)}, u32[]{:S(2)}) collective-permute-start(bf16[1,128,384]{2,1,0:T(8,128)(2,1)} %get-tuple-element.19), channel_id=1, source_target_pairs={{0,15},{1,2},{4,3},{5,6},{8,7},{9,10},{12,11},{13,14},{2,13},{3,0}... | collective-permute-start | bytes 294920 | tf_op jit(solution)/shard_map/ppermute | solution.py:487
  24.1 15.3 %collective-permute-start.4 = (bf16[2,128,384]{2,1,0:T(8,128)(2,1)}, bf16[2,128,384]{2,1,0:T(8,128)(2,1)S(1)}, u32[]{:S(2)}, u32[]{:S(2)}) collective-permute-start(bf16[2,128,384]{2,1,0:T(8,128)(2,1)} %get-tuple-element.18), channel_id=1, source_target_pairs={{0,2},{2,0},{1,3},{3,1},{4,6},{6,4},{5,7},{7,5},{8,10},{10,8},{9,1... | collective-permute-start | bytes 589832 | tf_op jit(solution)/shard_map/ppermute | solution.py:476
  24.6 14.8 %collective-permute-start.3 = (bf16[3,128,384]{2,1,0:T(8,128)(2,1)}, bf16[3,128,384]{2,1,0:T(8,128)(2,1)S(1)}, u32[]{:S(2)}, u32[]{:S(2)}) collective-permute-start(bf16[3,128,384]{2,1,0:T(8,128)(2,1)} %get-tuple-element.17), channel_id=1, source_target_pairs={{0,2},{2,0},{1,3},{3,1},{4,6},{6,4},{5,7},{7,5},{8,10},{10,8},{9,1... | collective-permute-start | bytes 884744 | tf_op jit(solution)/shard_map/ppermute | solution.py:476
  26.1 13.4 %collective-permute-start.2 = (bf16[4,224,384]{2,1,0:T(8,128)(2,1)}, bf16[4,224,384]{2,1,0:T(8,128)(2,1)S(1)}, u32[]{:S(2)}, u32[]{:S(2)}) collective-permute-start(bf16[4,224,384]{2,1,0:T(8,128)(2,1)} %get-tuple-element.16), channel_id=1, source_target_pairs={{0,13},{1,0},{4,1},{5,4},{8,5},{9,8},{12,9},{13,12},{2,15},{3,2},{... | collective-permute-start | bytes 2064392 | tf_op jit(solution)/shard_map/ppermute | solution.py:487
  53.3 14.5 %collective-permute-start.8 = (bf16[4,200,384]{2,1,0:T(8,128)(2,1)}, bf16[4,200,384]{2,1,0:T(8,128)(2,1)S(1)}, u32[]{:S(2)}, u32[]{:S(2)}) collective-permute-start(bf16[4,200,384]{2,1,0:T(8,128)(2,1)} %get-tuple-element.22), channel_id=1, source_target_pairs={{0,1},{1,4},{4,5},{5,8},{8,9},{9,12},{12,13},{13,0},{2,3},{3,6},{6... | collective-permute-start | bytes 1843208 | tf_op jit(solution)/shard_map/ppermute | solution.py:487
  53.9 34.6 %collective-permute-start.6 = (bf16[8,200,384]{2,1,0:T(8,128)(2,1)}, bf16[8,200,384]{2,1,0:T(8,128)(2,1)S(1)}, u32[]{:S(2)}, u32[]{:S(2)}) collective-permute-start(bf16[8,200,384]{2,1,0:T(8,128)(2,1)} %get-tuple-element.20.refs_0_), channel_id=1, source_target_pairs={{0,1},{1,0},{2,3},{3,2},{4,5},{5,4},{6,7},{7,6},{8,9},{9,8},{10,11... | collective-permute-start | bytes 3686408 | tf_op jit(solution)/shard_map/ppermute | solution.py:476
  53.9 14.0 %copy-start.15 = (bf16[1,104,384]{2,1,0:T(8,128)(2,1)S(1)}, bf16[1,104,384]{2,1,0:T(8,128)(2,1)}, u32[]{:S(2)}) copy-start(bf16[1,104,384]{2,1,0:T(8,128)(2,1)} %get-tuple-element.21.refs_5_) | copy-start | bytes 239620
  53.9 20.5 %copy-start.13 = (bf16[2,112,384]{2,1,0:T(8,128)(2,1)S(1)}, bf16[2,112,384]{2,1,0:T(8,128)(2,1)}, u32[]{:S(2)}) copy-start(bf16[2,112,384]{2,1,0:T(8,128)(2,1)} %get-tuple-element.23) | copy-start | bytes 516100
  67.3 21.1 %collective-permute-start.7 = (bf16[8,200,384]{2,1,0:T(8,128)(2,1)}, bf16[8,200,384]{2,1,0:T(8,128)(2,1)S(1)}, u32[]{:S(2)}, u32[]{:S(2)}) collective-permute-start(bf16[8,200,384]{2,1,0:T(8,128)(2,1)} %shard_map.58.refs_1_), channel_id=1, source_target_pairs={{0,1},{1,0},{2,3},{3,2},{4,5},{5,4},{6,7},{7,6},{8,9},{9,8},{10,11... | collective-permute-start | bytes 3686408 | tf_op jit(solution)/shard_map/ppermute | solution.py:476
  67.8 17.0 %copy-start.3 = (bf16[4,200,384]{2,1,0:T(8,128)(2,1)}, bf16[4,200,384]{2,1,0:T(8,128)(2,1)S(1)}, u32[]{:S(2)}) copy-start(bf16[4,200,384]{2,1,0:T(8,128)(2,1)S(1)} %collective-permute-done.8.refs_2_) | copy-start | bytes 1843204
  67.8 20.6 %collective-permute-start.9 = (bf16[4,200,384]{2,1,0:T(8,128)(2,1)S(1)}, bf16[4,200,384]{2,1,0:T(8,128)(2,1)S(1)}, u32[]{:S(2)}, u32[]{:S(2)}) collective-permute-start(bf16[4,200,384]{2,1,0:T(8,128)(2,1)S(1)} %collective-permute-done.8.refs_2_), channel_id=1, source_target_pairs={{0,1},{1,0},{2,3},{3,2},{4,5},{5,4},{6,7},{7,6},{8,9},{9,8},{10,11... | collective-permute-start | bytes 1843208 | tf_op jit(solution)/shard_map/ppermute | solution.py:476
  67.9 6.5 %collective-permute-start.14 = (bf16[1,104,384]{2,1,0:T(8,128)(2,1)S(1)}, bf16[1,104,384]{2,1,0:T(8,128)(2,1)S(1)}, u32[]{:S(2)}, u32[]{:S(2)}) collective-permute-start(bf16[1,104,384]{2,1,0:T(8,128)(2,1)S(1)} %copy-done.15), channel_id=1, source_target_pairs={{0,3},{1,6},{4,7},{5,10},{8,11},{9,14},{12,15},{13,2},{2,1},{3,4},... | collective-permute-start | bytes 239624 | tf_op jit(solution)/shard_map/ppermute | solution.py:487
  74.5 2.1 %copy-start.7 = (bf16[1,104,384]{2,1,0:T(8,128)(2,1)}, bf16[1,104,384]{2,1,0:T(8,128)(2,1)S(1)}, u32[]{:S(2)}) copy-start(bf16[1,104,384]{2,1,0:T(8,128)(2,1)S(1)} %collective-permute-done.14.refs_5_) | copy-start | bytes 239620
  74.5 1.3 %collective-permute-start.15 = (bf16[1,104,384]{2,1,0:T(8,128)(2,1)S(1)}, bf16[1,104,384]{2,1,0:T(8,128)(2,1)S(1)}, u32[]{:S(2)}, u32[]{:S(2)}) collective-permute-start(bf16[1,104,384]{2,1,0:T(8,128)(2,1)S(1)} %collective-permute-done.14.refs_5_), channel_id=1, source_target_pairs={{0,1},{1,0},{2,3},{3,2},{4,5},{5,4},{6,7},{7,6},{8,9},{9,8},{10,11... | collective-permute-start | bytes 239624 | tf_op jit(solution)/shard_map/ppermute | solution.py:476
  74.5 7.3 %collective-permute-start.10 = (bf16[2,112,384]{2,1,0:T(8,128)(2,1)S(1)}, bf16[2,112,384]{2,1,0:T(8,128)(2,1)S(1)}, u32[]{:S(2)}, u32[]{:S(2)}) collective-permute-start(bf16[2,112,384]{2,1,0:T(8,128)(2,1)S(1)} %copy-done.13), channel_id=1, source_target_pairs={{0,2},{2,0},{1,3},{3,1},{4,6},{6,4},{5,7},{7,5},{8,10},{10,8},{9,1... | collective-permute-start | bytes 516104 | tf_op jit(solution)/shard_map/ppermute | solution.py:476
  75.7 12.7 %copy-start.6 = (bf16[1,104,384]{2,1,0:T(8,128)(2,1)}, bf16[1,104,384]{2,1,0:T(8,128)(2,1)S(1)}, u32[]{:S(2)}) copy-start(bf16[1,104,384]{2,1,0:T(8,128)(2,1)S(1)} %collective-permute-done.15.refs_5_) | copy-start | bytes 239620
  75.7 9.0 %collective-permute-start.12 = (bf16[2,104,384]{2,1,0:T(8,128)(2,1)}, bf16[2,104,384]{2,1,0:T(8,128)(2,1)}, u32[]{:S(2)}, u32[]{:S(2)}) collective-permute-start(bf16[2,104,384]{2,1,0:T(8,128)(2,1)} %get-tuple-element.24), channel_id=1, source_target_pairs={{0,2},{2,0},{1,3},{3,1},{4,6},{6,4},{5,7},{7,5},{8,10},{10,8},{9,1... | collective-permute-start | bytes 479240 | tf_op jit(solution)/shard_map/ppermute | solution.py:476
  81.8 3.0 %copy-start.5 = (bf16[2,112,384]{2,1,0:T(8,128)(2,1)}, bf16[2,112,384]{2,1,0:T(8,128)(2,1)S(1)}, u32[]{:S(2)}) copy-start(bf16[2,112,384]{2,1,0:T(8,128)(2,1)S(1)} %collective-permute-done.10.refs_3_) | copy-start | bytes 516100
  81.8 6.6 %collective-permute-start.11 = (bf16[2,112,384]{2,1,0:T(8,128)(2,1)S(1)}, bf16[2,112,384]{2,1,0:T(8,128)(2,1)S(1)}, u32[]{:S(2)}, u32[]{:S(2)}) collective-permute-start(bf16[2,112,384]{2,1,0:T(8,128)(2,1)S(1)} %collective-permute-done.10.refs_3_), channel_id=1, source_target_pairs={{0,1},{1,0},{2,3},{3,2},{4,5},{5,4},{6,7},{7,6},{8,9},{9,8},{10,11... | collective-permute-start | bytes 516104 | tf_op jit(solution)/shard_map/ppermute | solution.py:476
  84.8 3.6 %collective-permute-start.13 = (bf16[2,104,384]{2,1,0:T(8,128)(2,1)}, bf16[2,104,384]{2,1,0:T(8,128)(2,1)}, u32[]{:S(2)}, u32[]{:S(2)}) collective-permute-start(bf16[2,104,384]{2,1,0:T(8,128)(2,1)} %collective-permute-done.12.refs_4_), channel_id=1, source_target_pairs={{0,1},{1,0},{2,3},{3,2},{4,5},{5,4},{6,7},{7,6},{8,9},{9,8},{10,11... | collective-permute-start | bytes 479240 | tf_op jit(solution)/shard_map/ppermute | solution.py:476
  88.4 1.3 %copy-start = (bf16[8,200,384]{2,1,0:T(8,128)(2,1)}, bf16[8,200,384]{2,1,0:T(8,128)(2,1)S(1)}, u32[]{:S(2)}) copy-start(bf16[8,200,384]{2,1,0:T(8,128)(2,1)S(1)} %collective-permute-done.6.refs_0_) | copy-start | bytes 3686404
  89.7 1.0 %copy-start.1 = (bf16[8,200,384]{2,1,0:T(8,128)(2,1)}, bf16[8,200,384]{2,1,0:T(8,128)(2,1)S(1)}, u32[]{:S(2)}) copy-start(bf16[8,200,384]{2,1,0:T(8,128)(2,1)S(1)} %collective-permute-done.7.refs_1_) | copy-start | bytes 3686404
  (8 other events, 6.2 us)
where the time goes:
time: 94.8 us; the launch traced here: 94.4 us
  Pallas kernels  59.5 us (63%)
  waiting for transfers between devices  17.6 us (19%)
  starting transfers between devices  11.4 us (12%)
  local copies, waits for them, and re-layouts  5.59 us (6%)
    pallas_call x2, Pallas kernels, first_call(): call(functools.partial(first_kernel, plan, which), specs, outs, scratch,...  26.9 us
    pallas_call x2, Pallas kernels, second_call(): call(functools.partial(second_kernel, plan, which, d), [ANY] * len(ins),...  25.5 us
    ppermute x12, waiting for transfers between devices, ring(): return lax.ppermute(value, tuple(axes), pairs)  11.6 us
    pallas_call x2, Pallas kernels, place_call(): call(functools.partial(place_kernel, plan, which, d), [ANY] * 6 + [HBM] *...  7.09 us
    ppermute x4, starting transfers between devices, beside(): lax.ppermute(value, axes, list(zip(line.ravel().tolist(), moved.ravel().t...  6.78 us
    ppermute x4, waiting for transfers between devices, beside(): lax.ppermute(value, axes, list(zip(line.ravel().tolist(), moved.ravel().t...  6.01 us
    unnamed x32, local copies, waits for them, and re-layouts  5.59 us
    ppermute x12, starting transfers between devices, ring(): return lax.ppermute(value, tuple(axes), pairs)  4.64 us
  transfers between devices with their start and end apart: 16, of which 5 were waited for; matrix products, arithmetic and copies ran while one was open for 0% of the time, Pallas kernels for 32%

commit v1 on v0

v1 whole, which is shorter than its diff:
```python
import functools

import jax
import jax.numpy as jnp
import numpy as np
from jax import lax
from jax.experimental import pallas as pl
from jax.experimental.pallas import tpu as pltpu
from jax.sharding import PartitionSpec as P


HD = 32
WH = 10
WW = 20
T = WH * WW
ROWS = 4
TP = 208
KP = 256
LIMIT = 20
BRING = 56
REC = 224
HALF = 112
SENT = HALF + 16
NEG = -1e30
SCALE = HD**-0.5 * 1.4426950408889634
f32 = jnp.float32
bf16 = jnp.bfloat16
NT = (((1,), (1,)), ((), ()))
HBM = pl.BlockSpec(memory_space=pltpu.HBM)
ANY = pl.BlockSpec(memory_space=pl.ANY)
VMEM = pl.BlockSpec(memory_space=pltpu.VMEM)


def normed(x):
    centred = x - jnp.mean(x, axis=-1, keepdims=True)
    variance = jnp.mean(centred * centred, axis=-1, keepdims=True)
    return (centred * lax.rsqrt(variance + 1e-05)).astype(bf16)


def blocks(pairs, load, again, land_rows, keeps, put, weights, slots, heads=4, ahead=1):
    wqk, wv, wout = weights
    d = wv.shape[0]
    lane = lax.broadcasted_iota(jnp.int32, (1, 128), 1)
    masks = [jnp.where((lane >= HD * j) & (lane < HD * j + HD), 1.0, 0.0).astype(bf16) for j in range(4)]
    unit = jnp.broadcast_to(jnp.where(lane == 0, 1.0, 0.0), (TP, 128)).astype(bf16)
    ones = jnp.ones((16, TP), bf16)
    total = len(pairs)

    def before(t):
        norm, qk, values, _, _, bias, land = slots[t % 2]

        def normal(i):
            norm[i * TP : i * TP + T, :] = normed(load(t, i))

        def mask():
            rows = land_rows(t)
            land[...] = jnp.transpose(jnp.concatenate(rows + [rows[0]] * 6, axis=0))
            for i in range(2):
                bias[i] = jnp.where(lane == 0, land[:TP, i : i + 1] * NEG, 0.0).astype(bf16)

        def project(at):
            wide = lax.broadcasted_iota(jnp.int32, (1, 256), 1) + at
            got = lax.dot_general(norm[...], wqk[at : at + 256], NT, preferred_element_type=f32)
            qk[:, at : at + 256] = (got * jnp.where(wide < d, SCALE, 1.0)).astype(bf16)

        def value(i):
            got = lax.dot_general(wv[...], norm[i * TP : i * TP + TP], NT, preferred_element_type=f32)
            values[i] = got.astype(bf16)

        return (
            [functools.partial(normal, i) for i in range(2)] + [mask]
            + [functools.partial(project, at) for at in range(0, 2 * d, 256)]
            + [functools.partial(value, i) for i in range(2)]
        )

    def after(t):
        _, _, _, mixed, joined, _, land = slots[t % 2]
        held = {}

        def turn(i):
            joined[i * TP : i * TP + TP] = jnp.transpose(mixed[i])

        def out():
            held["update"] = jnp.dot(joined[...], wout[...], preferred_element_type=f32)

        def add(i):
            keep = (1.0 - land[:T, i : i + 1]) * keeps(t, i)
            put(t, i, (again(t, i) + held["update"][i * TP : i * TP + T] * keep).astype(bf16))

        return [functools.partial(turn, i) for i in range(2)] + [out] + [functools.partial(add, i) for i in range(2)]

    units = [
        (t, i, g, tuple(range(a, a + heads)))
        for t in range(total) for i in range(2) for g in range(d // 128) for a in range(0, 4, heads)
    ]
    per = len(units) // total
    scores, probs = {}, {}

    def score(u):
        t, i, g, hs = units[u]
        qk, bias = slots[t % 2][1], slots[t % 2][5]
        k = qk[i * TP : i * TP + TP, d + 128 * g : d + 128 * g + 128]
        q = jnp.concatenate([qk[i * TP : i * TP + TP, 128 * g : 128 * g + 128], unit], axis=1)
        b = bias[i]
        keyed = jnp.concatenate([jnp.concatenate([k * masks[j], b], axis=1) for j in hs], axis=0)
        got = lax.dot_general(keyed, q, NT, preferred_element_type=f32)
        scores[u] = [got[n * TP : n * TP + TP] for n in range(len(hs))]

    def soften(u):
        probs[u] = [
            jnp.exp2((s - jnp.max(s, axis=0, keepdims=True)).astype(bf16)) for s in scores.pop(u)
        ]

    def mix(u):
        t, i, g, hs = units[u]
        values, mixed = slots[t % 2][2], slots[t % 2][3]
        for j, p in zip(hs, probs.pop(u)):
            at = 128 * g + HD * j
            both = jnp.dot(
                jnp.concatenate([values[i, at : at + HD], ones], axis=0), p, preferred_element_type=f32
            )
            mixed[i, at : at + HD] = (both[:HD] * (1.0 / both[HD : HD + 1])).astype(bf16)

    for piece in before(0):
        piece()
    pieces, step, place = [], 1.0, 1
    for k in range(len(units) + 2 * ahead):
        t, at = k // per, k % per
        if at == 2 * ahead:
            pieces = (after(t - 1) if t else []) + (before(t + 1) if t + 1 < total else [])
            step, place = (per - 2 * ahead) / (len(pieces) + 1), 1
        if k < len(units):
            score(k)
        if 0 <= k - ahead < len(units):
            soften(k - ahead)
        if 0 <= k - 2 * ahead:
            mix(k - 2 * ahead)
        while pieces and (at == per - 1 or at - 2 * ahead + 1 >= place * step):
            pieces.pop(0)()
            place += 1
    for piece in pieces + after(total - 1):
        piece()


def paired(windows):
    padded = list(windows) + [windows[-1]] * (len(windows) % 2)
    return [padded[n : n + 2] for n in range(0, len(padded), 2)]


def join_weights(block, sources, weights):
    wqk, wv, wout = weights
    for n in range(2):
        qkv, out = sources[2 * n : 2 * n + 2]
        half = out.shape[1]
        rows = slice(n * half, n * half + half)
        for part in range(2):
            wqk[part * 2 * half + n * half : part * 2 * half + n * half + half] = qkv[block, part]
        wv[rows] = qkv[block, 2]
        wout[rows] = out[block]


def clear_pads(slots):
    for slot in slots:
        for i in range(2):
            slot[0][i * TP + TP - 16 : i * TP + TP, :] = jnp.zeros((16, slot[0].shape[1]), bf16)


LOW = T - HALF + 8
MID = T // 2 // 16 * 16


def side_masks(left):
    token = lax.broadcasted_iota(jnp.int32, left.shape, 0)
    left[...] = jnp.where(token % WW < WW // 2, 1.0, 0.0).astype(bf16)


def merged(at, left, d):
    def pick(below, lo, hi):
        side = jnp.concatenate([left[lo:hi]] * (d // 128), axis=1) > 0.5
        return jnp.where(side, at(1, below, slice(lo, hi)), at(0, below, slice(lo, hi)))

    row = lax.broadcasted_iota(jnp.int32, (HALF - MID, d), 0) + MID
    middle = jnp.where(row < T // 2, pick(1, MID, HALF).astype(f32), pick(0, MID, HALF).astype(f32)).astype(bf16)
    return jnp.concatenate([pick(1, 0, MID), middle, pick(0, HALF, T)], axis=0)


class Plan:
    def __init__(self, columns):
        self.c = c = columns
        self.low = low = (c + 1) // 2
        self.up = c > low
        last = ROWS - 1
        sent = [(0, r) for r in range(ROWS)]
        sent += [(x, 0) for x in range(1, min(low, c - 1) + 1)]
        sent += [(x, last) for x in range(max(low, 1), c)]
        self.first_a = sent
        self.first_b = [(x, r) for x in range(c) for r in range(ROWS) if (x, r) not in sent]
        self.to_left = [(0, r) for r in range(ROWS)]
        self.to_above = [(x, 0) for x in range(min(low, c - 1) + 1)]
        self.to_below = [(x, last) for x in range(low, c)]
        self.to_diag = (0, last) if self.up else (0, 0)
        self.rim = [(c - 1, r) for r in range(last)]
        self.lower = [(x, last) for x in range(low)]
        self.upper = [(x, -1) for x in range(low, c)]
        self.inner = [(x, r) for x in range(c - 1) for r in range(last)]
        self.extra = len(self.rim) % 2 if self.inner else 0
        self.some = self.rim + self.inner[: self.extra]
        self.rest = self.inner[self.extra :]
        self.back_right = [(c - 1, r) for r in (range(-1, last) if self.up else range(ROWS))]

    def index(self, window):
        return window[0] * ROWS + window[1]


def bring_kernel(plan, *refs):
    sources, ends, sem = refs[:5], refs[5:10], refs[10]
    start = lax.axis_index("sub") * (plan.c * ROWS)
    pairs = [(sources[0].at[pl.ds(start, plan.c * ROWS)], ends[0])] + list(zip(sources[1:], ends[1:]))
    copies = [pltpu.make_async_copy(a, b, sem.at[n]) for n, (a, b) in enumerate(pairs)]
    for copy in copies:
        copy.start()
    for copy in copies:
        copy.wait()


def first_kernel(plan, which, *refs):
    windows = plan.first_b if which else plan.first_a
    tokens, land, ocean = refs[:3]
    sources, refs = refs[3:7], refs[7:]
    out, refs = refs[0], refs[1:]
    if which == 0:
        left, above, below, diag = refs[:4]
        refs = refs[4:]
    bits, weights, slots = refs[0], refs[1:4], (refs[4:11], refs[11:18])
    pairs = paired(list(range(len(windows))))
    start = lax.axis_index("sub") * (plan.c * ROWS)
    clear_pads(slots)
    bits[...] = jnp.ones(bits.shape, f32)
    bits[:, :T] = land[...].astype(f32)
    join_weights(0, sources, weights)

    def row(j):
        return bits[pl.ds(start + plan.index(windows[j]), 1), :]

    def listed(j):
        ident = lax.axis_index("lon") * (plan.c * ROWS * lax.axis_size("sub")) + start + plan.index(windows[j])
        return jnp.max(jnp.where(ocean[...] == ident, 1.0, 0.0), axis=1, keepdims=True)

    def put(t, i, value):
        j = pairs[t][i]
        w = windows[j]
        bottom = jnp.broadcast_to(row(j).astype(bf16), (REC - TP, KP))
        ends = [(out, j, 0)]
        if which == 0:
            ends += [(left, k, 0) for k, v in enumerate(plan.to_left) if v == w]
        for to, k, _ in ends:
            to[k, :T, :] = value
            to[k, TP:, :KP] = bottom
        if which == 0:
            halves = [(above, k, 0) for k, v in enumerate(plan.to_above) if v == w]
            halves += [(below, k, LOW) for k, v in enumerate(plan.to_below) if v == w]
            if w == plan.to_diag:
                halves.append((diag, 0, LOW if plan.up else 0))
            for to, k, at in halves:
                end = min(at + HALF, T)
                to[k, : end - at, :] = value[at:end]
                to[k, HALF:, :KP] = bottom[: SENT - HALF]

    def load(t, i):
        return tokens[plan.index(windows[pairs[t][i]])].astype(f32)

    blocks(
        pairs, load, load, lambda t: [row(j) for j in pairs[t]], lambda t, i: listed(pairs[t][i]), put, weights, slots
    )


def second_kernel(plan, which, d, *refs):
    firsts = refs[: 2 if plan.first_b else 1]
    refs = refs[len(firsts) :]
    sources, refs = refs[:4], refs[4 + which :]
    if which == 0:
        right, above, below, diag = refs[:4]
        refs = refs[4:]
    out, refs = refs[0], refs[1:]
    if which == 0:
        to_right, to_below, to_above, to_diag = refs[:4]
        refs = refs[4:]
    kept, left = refs[:2]
    weights, slots = refs[2:5], (refs[5:12], refs[12:19])
    side_masks(left)
    clear_pads(slots)
    join_weights(1, sources, weights)
    c = plan.c
    windows = plan.rest if which else plan.some
    all_windows = list(windows) if which else windows + plan.lower + plan.upper

    def record(x, r):
        if r == ROWS:
            return (above, x, 0, HALF) if x < len(plan.to_above) else (diag, 0, 0, HALF)
        if r < 0:
            return (below, x - plan.low, LOW, HALF) if x < c else (diag, 0, LOW, HALF)
        if x == c:
            return right, r, 0, TP
        if (x, r) in plan.first_a:
            return firsts[0], plan.first_a.index((x, r)), 0, TP
        return firsts[1], plan.first_b.index((x, r)), 0, TP

    token = lax.broadcasted_iota(jnp.int32, (1, KP), 1)
    left_row, top_row = token % WW < WW // 2, token < T // 2

    def gathered(x, r):
        def at(i, j, rows):
            ref, k, base, _ = record(x + i, r + j)
            return ref[k, rows.start - base : rows.stop - base, :]

        return merged(at, left, d)

    def land_of(x, r):
        a, b, e, f = [
            ref[k, at : at + 16, :KP].astype(f32)[:1]
            for ref, k, _, at in (record(x + i, r + j) for j in (0, 1) for i in (0, 1))
        ]
        return jnp.where(
            token < T, jnp.where(top_row, jnp.where(left_row, f, e), jnp.where(left_row, b, a)), 1.0
        )

    def store(n, value):
        out[n] = value
        if which:
            return
        w = all_windows[n]
        if w in plan.back_right:
            to_right[plan.back_right.index(w)] = value
        if w in plan.lower:
            to_below[plan.lower.index(w)] = value[:HALF]
        if w in plan.upper:
            to_above[plan.upper.index(w)] = value[LOW:]
        if w == (plan.back_right[0] if plan.up else plan.back_right[-1]):
            to_diag[0] = value[LOW:] if plan.up else value[:HALF]

    band, bands = lax.axis_index("lat"), lax.axis_size("lat")
    base = len(windows)
    lower_set = band < bands - 1 if plan.up else band >= 0
    on = jnp.where(lower_set, band < bands - 1, band > 0).astype(f32)

    def either(a, b):
        return jnp.where(lower_set, a.astype(f32), b.astype(f32)).astype(a.dtype)

    def window(place):
        if place[0] != "set":
            return gathered(*place)
        j = place[1]
        low = gathered(*plan.lower[j])
        return either(low, gathered(*plan.upper[min(j, len(plan.upper) - 1)])) if plan.up else low

    def land(place):
        if place[0] != "set":
            return land_of(*place)
        j = place[1]
        low = land_of(*plan.lower[j])
        return either(low, land_of(*plan.upper[min(j, len(plan.upper) - 1)])) if plan.up else low

    def finish(place, value):
        if place[0] != "set":
            return store(all_windows.index(place), value)
        j = place[1]
        if not plan.up:
            return store(base + j, value)
        store(base + j, either(value, gathered(*plan.lower[j])))
        if j < len(plan.upper):
            store(base + len(plan.lower) + j, either(gathered(*plan.upper[j]), value))

    def run(places, keep):
        pairs = paired(places)

        def load(t, i):
            value = window(pairs[t][i])
            kept[2 * (t % 3) + i] = value
            return value.astype(f32)

        def again(t, i):
            return kept[2 * (t % 3) + i].astype(f32)

        blocks(
            pairs, load, again, lambda t: [land(p) for p in pairs[t]], lambda t, i: keep(pairs[t][i]),
            lambda t, i, value: finish(pairs[t][i], value), weights, slots,
        )

    moving = [] if which else [("set", j) for j in range(len(plan.lower))]
    run(list(windows) + moving, lambda place: on if place[0] == "set" else 1.0)
    if which == 0 and plan.up and bands > 2:

        @pl.when((band > 0) & (band < bands - 1))
        def _():
            run(plan.upper, lambda place: 1.0)


def place_kernel(plan, which, d, *refs):
    raw_c, raw_d, lefts, aboves, belows, corner = refs[:6]
    out, fin, left, sem_out = refs[6 + which :]
    c = plan.c
    side_masks(left)
    where = {}
    for j, w in enumerate(plan.some + plan.lower + plan.upper):
        where[w] = (raw_c, j, 0)
    for j, w in enumerate(plan.rest):
        where[w] = (raw_d, j, 0)
    for k, (_, r) in enumerate(plan.back_right):
        where[-1, r] = (lefts, k, 0)
    for k, (x, _) in enumerate(plan.lower):
        where[x, -1] = (aboves, k, 0)
    for k, (x, _) in enumerate(plan.upper):
        where[x, ROWS - 1] = (belows, k, LOW)
    where[(-1, ROWS - 1) if plan.up else (-1, -1)] = (corner, 0, LOW if plan.up else 0)
    me = lax.axis_index("sub")
    start = (1 - me if which else me) * (c * ROWS)
    copies = []
    for x in range(c):
        for r in range(ROWS):
            w = x * ROWS + r

            def at(i, j, rows, x=x, r=r):
                ref, k, base = where[x - i, r - j]
                return ref[k, rows.start - base : rows.stop - base, :]

            fin[w] = merged(at, left, d)
            copies.append(pltpu.make_async_copy(fin.at[w], out.at[start + w], sem_out.at[w]))
            copies[-1].start()
    for copy in copies:
        copy.wait()


def ring(value, axes, by):
    sizes = [lax.axis_size(a) for a in axes]
    total = int(np.prod(sizes))
    grid = np.arange(total).reshape(sizes)
    moved = grid
    for dim, step in enumerate(by):
        moved = np.roll(moved, -step, axis=dim)
    pairs = list(zip(grid.ravel().tolist(), moved.ravel().tolist()))
    return lax.ppermute(value, tuple(axes), pairs)


def beside(value, lat, step):
    lon, sub, lats = lax.axis_size("lon"), lax.axis_size("sub"), lax.axis_size("lat")
    ident = np.arange(lon * lats * sub).reshape(lon, lats, sub)
    line = np.transpose(ident, (1, 0, 2)).reshape(lats, lon * sub)
    axes = ("lon", "lat", "sub")
    if not lat:
        line, axes = np.arange(lon * sub)[None], ("lon", "sub")
    moved = np.roll(line, (-lat, -step), axis=(0, 1))
    return lax.ppermute(value, axes, list(zip(line.ravel().tolist(), moved.ravel().tolist())))


def call(body, ins, outs, scratch, alias, flops, limit, where):
    total = sum(int(np.prod(o.shape)) * 2 for o in outs)
    return pl.pallas_call(
        body, in_specs=ins, out_specs=[where] * len(outs), out_shape=outs, scratch_shapes=scratch,
        input_output_aliases=alias,
        compiler_params=pltpu.CompilerParams(vmem_limit_bytes=limit * 2**20),
        cost_estimate=pl.CostEstimate(flops=flops, bytes_accessed=2 * total, transcendentals=0),
    )


def shards(tokens, land_bits, ocean_list, w_qkv, w_out):
    window_count, _, d = tokens.shape
    mine = window_count // lax.axis_size("sub")
    plan = Plan(mine // ROWS)
    turned = jnp.swapaxes(w_qkv, 2, 3)
    other_qkv, other_out = ring((turned, w_out), ("sub",), (1,))
    per_window = 12_000_000_000

    def shape(*s):
        return jax.ShapeDtypeStruct(s, bf16)

    def like(a):
        return jax.ShapeDtypeStruct(a.shape, a.dtype)

    own = call(
        functools.partial(bring_kernel, plan), [ANY] * 5,
        [shape(mine, T, d), like(land_bits), like(ocean_list), like(turned), like(w_out)],
        [pltpu.SemaphoreType.DMA((5,))], {}, 1_000_000, BRING, VMEM,
    )(tokens, land_bits, ocean_list, turned, w_out)
    weights = (own[3], own[4], other_qkv, other_out)
    slot = [
        pltpu.VMEM((2 * TP, d), bf16), pltpu.VMEM((2 * TP, 2 * d), bf16), pltpu.VMEM((2, d, TP), bf16),
        pltpu.VMEM((2, d, TP), bf16), pltpu.VMEM((2 * TP, d), bf16), pltpu.VMEM((2, TP, 128), bf16),
        pltpu.VMEM((KP, 8), f32),
    ]
    work = [pltpu.VMEM((2 * d, d), bf16), pltpu.VMEM((d, d), bf16), pltpu.VMEM((d, d), bf16)] + slot + slot

    def first_call(which, outs):
        n = len(plan.first_b if which else plan.first_a)
        return call(
            functools.partial(first_kernel, plan, which), [VMEM] * 7, outs,
            [pltpu.VMEM((window_count, KP), f32)] + work, {}, n * per_window, LIMIT, VMEM,
        )(*own[:3], *weights)

    halves = [shape(n, SENT, d) for n in (len(plan.to_above), max(len(plan.to_below), 1), 1)]
    first_a, left, above, below, diag = first_call(
        0, [shape(len(plan.first_a), REC, d), shape(ROWS, REC, d)] + halves
    )
    right = beside(left, 0, -1)
    from_below = ring(above, ("lat",), (-1,))
    from_above = ring(below, ("lat",), (1,)) if plan.up else below
    from_diag = beside(diag, 1 if plan.up else -1, -1)
    firsts = (first_a,)
    if plan.first_b:
        firsts += tuple(first_call(1, [shape(len(plan.first_b), REC, d)]))

    def second_call(which, ins, outs):
        scratch = [pltpu.VMEM((6, T, d), bf16), pltpu.VMEM((T, 128), bf16)] + work
        return call(
            functools.partial(second_kernel, plan, which, d), [VMEM] * len(ins), outs, scratch,
            {}, outs[0].shape[0] * per_window, LIMIT, VMEM,
        )(*ins)

    rim = len(plan.some) + len(plan.lower) + len(plan.upper)
    raw_c, to_right, to_below, to_above, to_diag = second_call(
        0,
        firsts + weights + (right, from_below, from_above, from_diag),
        [
            shape(rim, T, d), shape(ROWS, T, d), shape(len(plan.lower), HALF, d),
            shape(max(len(plan.upper), 1), T - LOW, d), shape(1, T - LOW if plan.up else HALF, d),
        ],
    )
    lefts = beside(to_right, 0, 1)
    aboves = ring(to_below, ("lat",), (1,))
    belows = ring(to_above, ("lat",), (-1,)) if plan.up else to_above
    corner = beside(to_diag, -1 if plan.up else 1, 1)
    other_c = ring(raw_c, ("sub",), (1,))
    raw_d = raw_c
    if plan.rest:
        raw_d = second_call(1, firsts + weights + (to_diag,), [shape(len(plan.rest), T, d)])[0]
    other_d = ring(raw_d, ("sub",), (1,)) if plan.rest else other_c
    here = (lefts, aboves, belows, corner)
    there = ring(here, ("sub",), (1,))

    def place_call(which, *ins):
        return call(
            functools.partial(place_kernel, plan, which, d), [VMEM] * 6 + [HBM] * which,
            [shape(window_count, T, d)],
            [pltpu.VMEM((mine, T, d), bf16), pltpu.VMEM((T, 128), bf16), pltpu.SemaphoreType.DMA((mine,))],
            {6: 0} if which else {}, 100_000_000, LIMIT, HBM,
        )(*ins)[0]

    out = place_call(0, raw_c, raw_d, *here)
    return place_call(1, other_c, other_d, *there, out)


def solution(mesh):
    placed = (
        P(("groups", "lat", "lon"), None, None),
        P(("groups", "lat", "lon"), None),
        P(("groups", "lat"), None),
        P(None, None, None, "sub"),
        P(None, "sub", None),
    )
    return jax.shard_map(
        shards,
        mesh=mesh,
        in_specs=placed,
        out_specs=P(("groups", "lat", "lon"), None, None),
        check_vma=False,
    )
```

time: 94.8 us -> 75.2 us (0.79)
  Pallas kernels: 59.5 us -> 41.5 us
  waiting for transfers between devices: 17.6 us -> 13.3 us
  starting transfers between devices: 11.4 us -> 14.6 us
    pallas_call x6 -> x7, Pallas kernels: 59.5 us -> 41.5 us  [the longest x2 17.9 us: first_call(): call(functools.partial(first_kernel, plan, which), [VMEM] * 7, outs, [plt...]
    ppermute x12, waiting for transfers between devices: 11.6 us -> 7.83 us  [ring(): return lax.ppermute(value, tuple(axes), pairs)]
    ppermute x12, starting transfers between devices: 4.64 us -> 7.05 us  [ring(): return lax.ppermute(value, tuple(axes), pairs)]
    unnamed x32 -> x14, local copies, waits for them, and re-layouts: 5.59 us -> 5.15 us
  transfers between devices with their start and end apart: 16 -> 16, of which waited for: 5 -> 5; matrix products, arithmetic and copies ran while one was open for 0% -> 0% of each run, Pallas kernels for 32% -> 31%
where the time goes in v1:
time: 75.2 us; the launch traced here: 74.9 us
  Pallas kernels  41.5 us (55%)
  starting transfers between devices  14.6 us (19%)
  waiting for transfers between devices  13.3 us (18%)
  local copies, waits for them, and re-layouts  5.15 us (7%)
    pallas_call x2, Pallas kernels, first_call(): call(functools.partial(first_kernel, plan, which), [VMEM] * 7, outs, [plt...  17.9 us
    pallas_call x2, Pallas kernels, second_call(): call(functools.partial(second_kernel, plan, which, d), [VMEM] * len(ins),...  16.4 us
    ppermute x12, waiting for transfers between devices, ring(): return lax.ppermute(value, tuple(axes), pairs)  7.83 us
    ppermute x4, starting transfers between devices, beside(): lax.ppermute(value, axes, list(zip(line.ravel().tolist(), moved.ravel().t...  7.51 us
    ppermute x12, starting transfers between devices, ring(): return lax.ppermute(value, tuple(axes), pairs)  7.05 us
    ppermute x4, waiting for transfers between devices, beside(): lax.ppermute(value, axes, list(zip(line.ravel().tolist(), moved.ravel().t...  5.47 us
    unnamed x14, local copies, waits for them, and re-layouts  5.15 us
    pallas_call x1, Pallas kernels, shards(): call(functools.partial(bring_kernel, plan), [ANY] * 5, [shape(mine, T, d)...  3.88 us
  transfers between devices with their start and end apart: 16, of which 5 were waited for; matrix products, arithmetic and copies ran while one was open for 0% of the time, Pallas kernels for 31%

profile of v1, /device:TPU:0, one launch (start us, length us, event | category | flops | bytes accessed | tf_op | source)
XLA Modules:
  0.0 74.9 jit_solution(1973023256129232872)
XLA Ops:
  0.0 0.5 collective-permute-start
  0.5 3.9 %shard_map.55 = (bf16[16,200,384]{2,1,0:T(8,128)(2,1)}, s32[32,200]{1,0:T(8,128)}, s32[1,128]{1,0:T(1,128)}, bf16[2,3,192,384]{3,2,1,0:T(8,128)(2,1)}, bf16[2,192,384]{2,1,0:T(8,128)(2,1)}) custom-call(bf16[32,200,384]{2,1,0:T(8,128)(2,1)} %refs_0_.1, s32[32,200]{1,0:T(8,128)} %refs_1_.1, s32[1,128]{1,0:T(1,128)} %refs_2_.1, ...), custom_call_target="tpu_custom_call" | custom-call | flops 1000000 | bytes 7300608 | tf_op jit(solution)/shard_map/pallas_call | solution.py:479
  4.4 1.7 %copy-done = bf16[16,200,384]{2,1,0:T(8,128)(2,1)S(1)} copy-done((bf16[16,200,384]{2,1,0:T(8,128)(2,1)S(1)}, bf16[16,200,384]{2,1,0:T(8,128)(2,1)}, u32[]{:S(2)}) %copy-start) | copy-done | bytes 2457624
  6.1 1.2 %copy-done.1 = bf16[2,3,192,384]{3,2,1,0:T(8,128)(2,1)S(1)} copy-done((bf16[2,3,192,384]{3,2,1,0:T(8,128)(2,1)S(1)}, bf16[2,3,192,384]{3,2,1,0:T(8,128)(2,1)}, u32[]{:S(2)}) %copy-start.1) | copy-done | bytes 884760
  7.3 1.0 %copy-done.3 = bf16[2,192,384]{2,1,0:T(8,128)(2,1)S(1)} copy-done((bf16[2,192,384]{2,1,0:T(8,128)(2,1)S(1)}, bf16[2,192,384]{2,1,0:T(8,128)(2,1)}, u32[]{:S(2)}) %copy-start.3) | copy-done | bytes 294936
  8.3 0.8 %copy-done.5 = s32[32,200]{1,0:T(8,128)S(1)} copy-done((s32[32,200]{1,0:T(8,128)S(1)}, s32[32,200]{1,0:T(8,128)}, u32[]{:S(2)}) %copy-start.5) | copy-done | bytes 25624
  9.0 0.6 copy-done.6
  9.6 9.0 %shard_map.56 = (bf16[8,224,384]{2,1,0:T(8,128)(2,1)S(1)}, bf16[4,224,384]{2,1,0:T(8,128)(2,1)S(1)}, bf16[3,128,384]{2,1,0:T(8,128)(2,1)S(1)}, bf16[2,128,384]{2,1,0:T(8,128)(2,1)S(1)}, bf16[1,128,384]{2,1,0:T(8,128)(2,1)S(1)}) custom-call(bf16[16,200,384]{2,1,0:T(8,128)(2,1)S(1)} %copy-done, s32[32,200]{1,0:T(8,128)S(1)} %copy-done.5, ...), custom_call_target="tpu_custom_call" | custom-call | flops 96000000000 | bytes 5308416 | tf_op jit(solution)/shard_map/pallas_call | solution.py:494
  18.6 5.7 %collective-permute-start.5 = (bf16[1,128,384]{2,1,0:T(8,128)(2,1)S(1)}, bf16[1,128,384]{2,1,0:T(8,128)(2,1)S(1)}, u32[]{:S(2)}, u32[]{:S(2)}) collective-permute-start(bf16[1,128,384]{2,1,0:T(8,128)(2,1)S(1)} %get-tuple-element.29), channel_id=1, source_target_pairs={{0,15},{1,2},{4,3},{5,6},{8,7},{9,10},{12,11},{13,14},{2,13},{3,0}... | collective-permute-start | bytes 294920 | tf_op jit(solution)/shard_map/ppermute | solution.py:452
  24.2 0.5 collective-permute-start.4
  24.7 1.5 %collective-permute-start.3 = (bf16[3,128,384]{2,1,0:T(8,128)(2,1)S(1)}, bf16[3,128,384]{2,1,0:T(8,128)(2,1)S(1)}, u32[]{:S(2)}, u32[]{:S(2)}) collective-permute-start(bf16[3,128,384]{2,1,0:T(8,128)(2,1)S(1)} %get-tuple-element.27), channel_id=1, source_target_pairs={{0,2},{2,0},{1,3},{3,1},{4,6},{6,4},{5,7},{7,5},{8,10},{10,8},{9,1... | collective-permute-start | bytes 884744 | tf_op jit(solution)/shard_map/ppermute | solution.py:441
  26.4 8.9 %shard_map.57.refs_1_ = bf16[8,224,384]{2,1,0:T(8,128)(2,1)S(1)} custom-call(bf16[16,200,384]{2,1,0:T(8,128)(2,1)S(1)} %copy-done, s32[32,200]{1,0:T(8,128)S(1)} %copy-done.5, s32[1,128]{1,0:T(1,128)S(1)} %copy-done.6, bf16[2,3,192,384]{3,2,1,0:T(8,128)(2,1)S(1)} %copy-done.1, bf16[2,192,384]{2,1,0:T(8,128)(2,1)S(1)} %copy-done.3, ...), custom_call_target="tpu_custom_call" | custom-call | flops 96000000000 | bytes 2752512 | tf_op jit(solution)/shard_map/pallas_call | solution.py:494
  35.7 7.4 %shard_map.58 = (bf16[8,200,384]{2,1,0:T(8,128)(2,1)S(1)}, bf16[4,200,384]{2,1,0:T(8,128)(2,1)S(1)}, bf16[2,112,384]{2,1,0:T(8,128)(2,1)S(1)}, bf16[2,104,384]{2,1,0:T(8,128)(2,1)S(1)}, bf16[1,104,384]{2,1,0:T(8,128)(2,1)S(1)}) custom-call(bf16[8,224,384]{2,1,0:T(8,128)(2,1)S(1)} %get-tuple-element.25.refs_0_, bf16[8,224,384]{2,1,0:T(8,128)(2,1)S(1)} %shard_map.57.refs_1_, ...), custom_call_target="tpu_custom_call" | custom-call | flops 96000000000 | bytes 4509696 | tf_op jit(solution)/shard_map/pallas_call | solution.py:513
  43.2 1.7 %collective-permute-start.6 = (bf16[8,200,384]{2,1,0:T(8,128)(2,1)S(1)}, bf16[8,200,384]{2,1,0:T(8,128)(2,1)S(1)}, u32[]{:S(2)}, u32[]{:S(2)}) collective-permute-start(bf16[8,200,384]{2,1,0:T(8,128)(2,1)S(1)} %get-tuple-element.30.refs_0_), channel_id=1, source_target_pairs={{0,1},{1,0},{2,3},{3,2},{4,5},{5,4},{6,7},{7,6},{8,9},{9,8},{10,11... | collective-permute-start | bytes 3686408 | tf_op jit(solution)/shard_map/ppermute | solution.py:441
  44.9 9.0 %shard_map.59.refs_1_ = bf16[8,200,384]{2,1,0:T(8,128)(2,1)S(1)} custom-call(bf16[8,224,384]{2,1,0:T(8,128)(2,1)S(1)} %get-tuple-element.25.refs_0_, bf16[8,224,384]{2,1,0:T(8,128)(2,1)S(1)} %shard_map.57.refs_1_, bf16[2,3,192,384]{3,2,1,0:T(8,128)(2,1)S(1)} %copy-done.2, bf16[2,192,384]{2,1,0:T(8,128)(2,1)S(1)} %copy-done.4, ...), custom_call_target="tpu_custom_call" | custom-call | flops 96000000000 | bytes 2457600 | tf_op jit(solution)/shard_map/pallas_call | solution.py:513
  54.0 0.5 collective-permute-done.8.refs_2_
  54.5 1.6 %collective-permute-start.14 = (bf16[1,104,384]{2,1,0:T(8,128)(2,1)S(1)}, bf16[1,104,384]{2,1,0:T(8,128)(2,1)S(1)}, u32[]{:S(2)}, u32[]{:S(2)}) collective-permute-start(bf16[1,104,384]{2,1,0:T(8,128)(2,1)S(1)} %get-tuple-element.31.refs_6_), channel_id=1, source_target_pairs={{0,3},{1,6},{4,7},{5,10},{8,11},{9,14},{12,15},{13,2},{2,1},{3,4},... | collective-permute-start | bytes 239624 | tf_op jit(solution)/shard_map/ppermute | solution.py:452
  56.2 4.9 %collective-permute-done.14.refs_5_ = bf16[1,104,384]{2,1,0:T(8,128)(2,1)S(1)} collective-permute-done((bf16[1,104,384]{2,1,0:T(8,128)(2,1)S(1)}, bf16[1,104,384]{2,1,0:T(8,128)(2,1)S(1)}, u32[]{:S(2)}, u32[]{:S(2)}) %collective-permute-start.14) | collective-permute-done | bytes 79904 | tf_op jit(solution)/shard_map/ppermute | solution.py:452
  61.1 1.5 %collective-permute-start.10 = (bf16[2,112,384]{2,1,0:T(8,128)(2,1)S(1)}, bf16[2,112,384]{2,1,0:T(8,128)(2,1)S(1)}, u32[]{:S(2)}, u32[]{:S(2)}) collective-permute-start(bf16[2,112,384]{2,1,0:T(8,128)(2,1)S(1)} %get-tuple-element.33), channel_id=1, source_target_pairs={{0,2},{2,0},{1,3},{3,1},{4,6},{6,4},{5,7},{7,5},{8,10},{10,8},{9,1... | collective-permute-start | bytes 516104 | tf_op jit(solution)/shard_map/ppermute | solution.py:441
  62.6 1.3 %collective-permute-start.12 = (bf16[2,104,384]{2,1,0:T(8,128)(2,1)S(1)}, bf16[2,104,384]{2,1,0:T(8,128)(2,1)S(1)}, u32[]{:S(2)}, u32[]{:S(2)}) collective-permute-start(bf16[2,104,384]{2,1,0:T(8,128)(2,1)S(1)} %get-tuple-element.34), channel_id=1, source_target_pairs={{0,2},{2,0},{1,3},{3,1},{4,6},{6,4},{5,7},{7,5},{8,10},{10,8},{9,1... | collective-permute-start | bytes 479240 | tf_op jit(solution)/shard_map/ppermute | solution.py:441
  63.9 4.5 %collective-permute-done.10.refs_3_ = bf16[2,112,384]{2,1,0:T(8,128)(2,1)S(1)} collective-permute-done((bf16[2,112,384]{2,1,0:T(8,128)(2,1)S(1)}, bf16[2,112,384]{2,1,0:T(8,128)(2,1)S(1)}, u32[]{:S(2)}, u32[]{:S(2)}) %collective-permute-start.10) | collective-permute-done | bytes 172064 | tf_op jit(solution)/shard_map/ppermute | solution.py:441
  68.3 3.0 %collective-permute-done.12.refs_4_ = bf16[2,104,384]{2,1,0:T(8,128)(2,1)S(1)} collective-permute-done((bf16[2,104,384]{2,1,0:T(8,128)(2,1)S(1)}, bf16[2,104,384]{2,1,0:T(8,128)(2,1)S(1)}, u32[]{:S(2)}, u32[]{:S(2)}) %collective-permute-start.12) | collective-permute-done | bytes 159776 | tf_op jit(solution)/shard_map/ppermute | solution.py:441
  71.3 1.7 %shard_map.60.refs_6_ = bf16[32,200,384]{2,1,0:T(8,128)(2,1)} custom-call(bf16[8,200,384]{2,1,0:T(8,128)(2,1)S(1)} %get-tuple-element.30.refs_0_, bf16[8,200,384]{2,1,0:T(8,128)(2,1)S(1)} %shard_map.59.refs_1_, bf16[4,200,384]{2,1,0:T(8,128)(2,1)S(1)} %collective-permute-done.8.refs_2_, bf16[2,112,384]{2,1,0:T(8,128)(2,1)S(1)} %collective-permute-done.10.refs_3_, ...), custom_call_target="tpu_custom_call" | custom-call | flops 100000000 | bytes 9830400 | tf_op jit(solution)/shard_map/pallas_call | solution.py:540
  73.0 1.7 %shard_map.61 = bf16[32,200,384]{2,1,0:T(8,128)(2,1)} custom-call(bf16[8,200,384]{2,1,0:T(8,128)(2,1)S(1)} %collective-permute-done.6.refs_0_, bf16[8,200,384]{2,1,0:T(8,128)(2,1)S(1)} %collective-permute-done.7.refs_1_, bf16[4,200,384]{2,1,0:T(8,128)(2,1)S(1)} %collective-permute-done.9.refs_2_, ...), custom_call_target="tpu_custom_call", output_to_operand_aliasing={{}: (6, {})} | custom-call | flops 100000000 | bytes 9830400 | tf_op jit(solution)/shard_map/pallas_call | solution.py:540
  (29 shorter events, 0.7 us)
Async XLA Ops:
  0.0 4.4 %collective-permute-start = (bf16[2,3,192,384]{3,2,1,0:T(8,128)(2,1)}, bf16[2,3,192,384]{3,2,1,0:T(8,128)(2,1)S(1)}, u32[]{:S(2)}, u32[]{:S(2)}) collective-permute-start(bf16[2,3,192,384]{3,2,1,0:T(8,128)(2,1)} %bitcast.1), channel_id=1, source_target_pairs={{0,1},{1,0},{2,3},{3,2},{4,5},{5,4},{6,7},{7,6},{8,9},{9,8},{10,11... | collective-permute-start | bytes 2654216 | tf_op jit(solution)/shard_map/ppermute | solution.py:441
  0.5 3.9 %collective-permute-start.1 = (bf16[2,192,384]{2,1,0:T(8,128)(2,1)}, bf16[2,192,384]{2,1,0:T(8,128)(2,1)S(1)}, u32[]{:S(2)}, u32[]{:S(2)}) collective-permute-start(bf16[2,192,384]{2,1,0:T(8,128)(2,1)} %refs_4_.1), channel_id=1, source_target_pairs={{0,1},{1,0},{2,3},{3,2},{4,5},{5,4},{6,7},{7,6},{8,9},{9,8},{10,11... | collective-permute-start | bytes 884744 | tf_op jit(solution)/shard_map/ppermute | solution.py:441
  4.4 1.7 %copy-start = (bf16[16,200,384]{2,1,0:T(8,128)(2,1)S(1)}, bf16[16,200,384]{2,1,0:T(8,128)(2,1)}, u32[]{:S(2)}) copy-start(bf16[16,200,384]{2,1,0:T(8,128)(2,1)} %get-tuple-element.20.refs_0_) | copy-start | bytes 7372804
  6.1 1.2 %copy-start.1 = (bf16[2,3,192,384]{3,2,1,0:T(8,128)(2,1)S(1)}, bf16[2,3,192,384]{3,2,1,0:T(8,128)(2,1)}, u32[]{:S(2)}) copy-start(bf16[2,3,192,384]{3,2,1,0:T(8,128)(2,1)} %get-tuple-element.23.refs_3_.refs_2_) | copy-start | bytes 2654212
  7.3 1.0 %copy-start.3 = (bf16[2,192,384]{2,1,0:T(8,128)(2,1)S(1)}, bf16[2,192,384]{2,1,0:T(8,128)(2,1)}, u32[]{:S(2)}) copy-start(bf16[2,192,384]{2,1,0:T(8,128)(2,1)} %get-tuple-element.24.refs_4_.refs_3_) | copy-start | bytes 884740
  8.3 0.8 %copy-start.5 = (s32[32,200]{1,0:T(8,128)S(1)}, s32[32,200]{1,0:T(8,128)}, u32[]{:S(2)}) copy-start(s32[32,200]{1,0:T(8,128)} %get-tuple-element.21.refs_1_) | copy-start | bytes 76804
  9.0 0.6 copy-start.6
  18.6 16.8 %collective-permute-start.5 = (bf16[1,128,384]{2,1,0:T(8,128)(2,1)S(1)}, bf16[1,128,384]{2,1,0:T(8,128)(2,1)S(1)}, u32[]{:S(2)}, u32[]{:S(2)}) collective-permute-start(bf16[1,128,384]{2,1,0:T(8,128)(2,1)S(1)} %get-tuple-element.29), channel_id=1, source_target_pairs={{0,15},{1,2},{4,3},{5,6},{8,7},{9,10},{12,11},{13,14},{2,13},{3,0}... | collective-permute-start | bytes 294920 | tf_op jit(solution)/shard_map/ppermute | solution.py:452
  24.2 11.1 %collective-permute-start.4 = (bf16[2,128,384]{2,1,0:T(8,128)(2,1)S(1)}, bf16[2,128,384]{2,1,0:T(8,128)(2,1)S(1)}, u32[]{:S(2)}, u32[]{:S(2)}) collective-permute-start(bf16[2,128,384]{2,1,0:T(8,128)(2,1)S(1)} %get-tuple-element.28), channel_id=1, source_target_pairs={{0,2},{2,0},{1,3},{3,1},{4,6},{6,4},{5,7},{7,5},{8,10},{10,8},{9,1... | collective-permute-start | bytes 589832 | tf_op jit(solution)/shard_map/ppermute | solution.py:441
  24.7 11.0 %collective-permute-start.3 = (bf16[3,128,384]{2,1,0:T(8,128)(2,1)S(1)}, bf16[3,128,384]{2,1,0:T(8,128)(2,1)S(1)}, u32[]{:S(2)}, u32[]{:S(2)}) collective-permute-start(bf16[3,128,384]{2,1,0:T(8,128)(2,1)S(1)} %get-tuple-element.27), channel_id=1, source_target_pairs={{0,2},{2,0},{1,3},{3,1},{4,6},{6,4},{5,7},{7,5},{8,10},{10,8},{9,1... | collective-permute-start | bytes 884744 | tf_op jit(solution)/shard_map/ppermute | solution.py:441
  26.2 9.5 %copy-start.2 = (bf16[2,3,192,384]{3,2,1,0:T(8,128)(2,1)S(1)}, bf16[2,3,192,384]{3,2,1,0:T(8,128)(2,1)}, u32[]{:S(2)}) copy-start(bf16[2,3,192,384]{3,2,1,0:T(8,128)(2,1)} %get-tuple-element.23.refs_3_.refs_2_) | copy-start | bytes 2654212
  26.2 9.5 %copy-start.4 = (bf16[2,192,384]{2,1,0:T(8,128)(2,1)S(1)}, bf16[2,192,384]{2,1,0:T(8,128)(2,1)}, u32[]{:S(2)}) copy-start(bf16[2,192,384]{2,1,0:T(8,128)(2,1)} %get-tuple-element.24.refs_4_.refs_3_) | copy-start | bytes 884740
  26.3 9.5 %collective-permute-start.2 = (bf16[4,224,384]{2,1,0:T(8,128)(2,1)S(1)}, bf16[4,224,384]{2,1,0:T(8,128)(2,1)S(1)}, u32[]{:S(2)}, u32[]{:S(2)}) collective-permute-start(bf16[4,224,384]{2,1,0:T(8,128)(2,1)S(1)} %get-tuple-element.26), channel_id=1, source_target_pairs={{0,13},{1,0},{4,1},{5,4},{8,5},{9,8},{12,9},{13,12},{2,15},{3,2},{... | collective-permute-start | bytes 2064392 | tf_op jit(solution)/shard_map/ppermute | solution.py:452
  43.1 11.4 %collective-permute-start.8 = (bf16[4,200,384]{2,1,0:T(8,128)(2,1)S(1)}, bf16[4,200,384]{2,1,0:T(8,128)(2,1)S(1)}, u32[]{:S(2)}, u32[]{:S(2)}) collective-permute-start(bf16[4,200,384]{2,1,0:T(8,128)(2,1)S(1)} %get-tuple-element.32), channel_id=1, source_target_pairs={{0,1},{1,4},{4,5},{5,8},{8,9},{9,12},{12,13},{13,0},{2,3},{3,6},{6... | collective-permute-start | bytes 1843208 | tf_op jit(solution)/shard_map/ppermute | solution.py:452
  43.2 29.8 %collective-permute-start.6 = (bf16[8,200,384]{2,1,0:T(8,128)(2,1)S(1)}, bf16[8,200,384]{2,1,0:T(8,128)(2,1)S(1)}, u32[]{:S(2)}, u32[]{:S(2)}) collective-permute-start(bf16[8,200,384]{2,1,0:T(8,128)(2,1)S(1)} %get-tuple-element.30.refs_0_), channel_id=1, source_target_pairs={{0,1},{1,0},{2,3},{3,2},{4,5},{5,4},{6,7},{7,6},{8,9},{9,8},{10,11... | collective-permute-start | bytes 3686408 | tf_op jit(solution)/shard_map/ppermute | solution.py:441
  53.9 19.1 %collective-permute-start.7 = (bf16[8,200,384]{2,1,0:T(8,128)(2,1)S(1)}, bf16[8,200,384]{2,1,0:T(8,128)(2,1)S(1)}, u32[]{:S(2)}, u32[]{:S(2)}) collective-permute-start(bf16[8,200,384]{2,1,0:T(8,128)(2,1)S(1)} %shard_map.59.refs_1_), channel_id=1, source_target_pairs={{0,1},{1,0},{2,3},{3,2},{4,5},{5,4},{6,7},{7,6},{8,9},{9,8},{10,11... | collective-permute-start | bytes 3686408 | tf_op jit(solution)/shard_map/ppermute | solution.py:441
  54.5 18.4 %collective-permute-start.9 = (bf16[4,200,384]{2,1,0:T(8,128)(2,1)S(1)}, bf16[4,200,384]{2,1,0:T(8,128)(2,1)S(1)}, u32[]{:S(2)}, u32[]{:S(2)}) collective-permute-start(bf16[4,200,384]{2,1,0:T(8,128)(2,1)S(1)} %collective-permute-done.8.refs_2_), channel_id=1, source_target_pairs={{0,1},{1,0},{2,3},{3,2},{4,5},{5,4},{6,7},{7,6},{8,9},{9,8},{10,11... | collective-permute-start | bytes 1843208 | tf_op jit(solution)/shard_map/ppermute | solution.py:441
  54.5 6.5 %collective-permute-start.14 = (bf16[1,104,384]{2,1,0:T(8,128)(2,1)S(1)}, bf16[1,104,384]{2,1,0:T(8,128)(2,1)S(1)}, u32[]{:S(2)}, u32[]{:S(2)}) collective-permute-start(bf16[1,104,384]{2,1,0:T(8,128)(2,1)S(1)} %get-tuple-element.31.refs_6_), channel_id=1, source_target_pairs={{0,3},{1,6},{4,7},{5,10},{8,11},{9,14},{12,15},{13,2},{2,1},{3,4},... | collective-permute-start | bytes 239624 | tf_op jit(solution)/shard_map/ppermute | solution.py:452
  61.1 1.5 %collective-permute-start.15 = (bf16[1,104,384]{2,1,0:T(8,128)(2,1)S(1)}, bf16[1,104,384]{2,1,0:T(8,128)(2,1)S(1)}, u32[]{:S(2)}, u32[]{:S(2)}) collective-permute-start(bf16[1,104,384]{2,1,0:T(8,128)(2,1)S(1)} %collective-permute-done.14.refs_5_), channel_id=1, source_target_pairs={{0,1},{1,0},{2,3},{3,2},{4,5},{5,4},{6,7},{7,6},{8,9},{9,8},{10,11... | collective-permute-start | bytes 239624 | tf_op jit(solution)/shard_map/ppermute | solution.py:441
  61.1 7.2 %collective-permute-start.10 = (bf16[2,112,384]{2,1,0:T(8,128)(2,1)S(1)}, bf16[2,112,384]{2,1,0:T(8,128)(2,1)S(1)}, u32[]{:S(2)}, u32[]{:S(2)}) collective-permute-start(bf16[2,112,384]{2,1,0:T(8,128)(2,1)S(1)} %get-tuple-element.33), channel_id=1, source_target_pairs={{0,2},{2,0},{1,3},{3,1},{4,6},{6,4},{5,7},{7,5},{8,10},{10,8},{9,1... | collective-permute-start | bytes 516104 | tf_op jit(solution)/shard_map/ppermute | solution.py:441
  62.6 8.7 %collective-permute-start.12 = (bf16[2,104,384]{2,1,0:T(8,128)(2,1)S(1)}, bf16[2,104,384]{2,1,0:T(8,128)(2,1)S(1)}, u32[]{:S(2)}, u32[]{:S(2)}) collective-permute-start(bf16[2,104,384]{2,1,0:T(8,128)(2,1)S(1)} %get-tuple-element.34), channel_id=1, source_target_pairs={{0,2},{2,0},{1,3},{3,1},{4,6},{6,4},{5,7},{7,5},{8,10},{10,8},{9,1... | collective-permute-start | bytes 479240 | tf_op jit(solution)/shard_map/ppermute | solution.py:441
  68.3 4.6 %collective-permute-start.11 = (bf16[2,112,384]{2,1,0:T(8,128)(2,1)S(1)}, bf16[2,112,384]{2,1,0:T(8,128)(2,1)S(1)}, u32[]{:S(2)}, u32[]{:S(2)}) collective-permute-start(bf16[2,112,384]{2,1,0:T(8,128)(2,1)S(1)} %collective-permute-done.10.refs_3_), channel_id=1, source_target_pairs={{0,1},{1,0},{2,3},{3,2},{4,5},{5,4},{6,7},{7,6},{8,9},{9,8},{10,11... | collective-permute-start | bytes 516104 | tf_op jit(solution)/shard_map/ppermute | solution.py:441
  71.3 1.7 %collective-permute-start.13 = (bf16[2,104,384]{2,1,0:T(8,128)(2,1)S(1)}, bf16[2,104,384]{2,1,0:T(8,128)(2,1)S(1)}, u32[]{:S(2)}, u32[]{:S(2)}) collective-permute-start(bf16[2,104,384]{2,1,0:T(8,128)(2,1)S(1)} %collective-permute-done.12.refs_4_), channel_id=1, source_target_pairs={{0,1},{1,0},{2,3},{3,2},{4,5},{5,4},{6,7},{7,6},{8,9},{9,8},{10,11... | collective-permute-start | bytes 479240 | tf_op jit(solution)/shard_map/ppermute | solution.py:441

commit v2 on v1

--- a/solution.py
+++ b/solution.py
@@ -17,7 +17,7 @@
 TP = 208
 KP = 256
 LIMIT = 20
-BRING = 56
+BRING = 48
 REC = 224
 HALF = 112
 SENT = HALF + 16
@@ -185,7 +185,7 @@
 
 
 class Plan:
-    def __init__(self, columns):
+    def __init__(self, columns, bands):
         self.c = c = columns
         self.low = low = (c + 1) // 2
         self.up = c > low
@@ -206,21 +206,18 @@
         self.extra = len(self.rim) % 2 if self.inner else 0
         self.some = self.rim + self.inner[: self.extra]
         self.rest = self.inner[self.extra :]
+        self.joined = self.up and bands == 2
         self.back_right = [(c - 1, r) for r in (range(-1, last) if self.up else range(ROWS))]
 
     def index(self, window):
         return window[0] * ROWS + window[1]
 
 
-def bring_kernel(plan, *refs):
-    sources, ends, sem = refs[:5], refs[5:10], refs[10]
+def bring_kernel(plan, tokens, land, ocean, qkv, out, mine, sem):
     start = lax.axis_index("sub") * (plan.c * ROWS)
-    pairs = [(sources[0].at[pl.ds(start, plan.c * ROWS)], ends[0])] + list(zip(sources[1:], ends[1:]))
-    copies = [pltpu.make_async_copy(a, b, sem.at[n]) for n, (a, b) in enumerate(pairs)]
-    for copy in copies:
-        copy.start()
-    for copy in copies:
-        copy.wait()
+    copy = pltpu.make_async_copy(tokens.at[pl.ds(start, plan.c * ROWS)], mine, sem)
+    copy.start()
+    copy.wait()
 
 
 def first_kernel(plan, which, *refs):
@@ -228,9 +225,11 @@
     tokens, land, ocean = refs[:3]
     sources, refs = refs[3:7], refs[7:]
     out, refs = refs[0], refs[1:]
-    if which == 0:
-        left, above, below, diag = refs[:4]
-        refs = refs[4:]
+    if which == 0 and plan.joined:
+        (left, above, diag), refs = refs[:3], refs[3:]
+        below = above
+    elif which == 0:
+        (left, above, below, diag), refs = refs[:4], refs[4:]
     bits, weights, slots = refs[0], refs[1:4], (refs[4:11], refs[11:18])
     pairs = paired(list(range(len(windows))))
     start = lax.axis_index("sub") * (plan.c * ROWS)
@@ -258,7 +257,8 @@
             to[k, TP:, :KP] = bottom
         if which == 0:
             halves = [(above, k, 0) for k, v in enumerate(plan.to_above) if v == w]
-            halves += [(below, k, LOW) for k, v in enumerate(plan.to_below) if v == w]
+            skip = len(plan.to_above) if plan.joined else 0
+            halves += [(below, skip + k, LOW) for k, v in enumerate(plan.to_below) if v == w]
             if w == plan.to_diag:
                 halves.append((diag, 0, LOW if plan.up else 0))
             for to, k, at in halves:
@@ -278,13 +278,18 @@
     firsts = refs[: 2 if plan.first_b else 1]
     refs = refs[len(firsts) :]
     sources, refs = refs[:4], refs[4 + which :]
-    if which == 0:
-        right, above, below, diag = refs[:4]
-        refs = refs[4:]
+    if which == 0 and plan.joined:
+        (right, above, diag), refs = refs[:3], refs[3:]
+        below = above
+    elif which == 0:
+        (right, above, below, diag), refs = refs[:4], refs[4:]
     out, refs = refs[0], refs[1:]
-    if which == 0:
-        to_right, to_below, to_above, to_diag = refs[:4]
-        refs = refs[4:]
+    if which == 0 and plan.joined:
+        (to_right, to_below, to_diag), refs = refs[:3], refs[3:]
+        to_above = to_below
+    elif which == 0:
+        (to_right, to_below, to_above, to_diag), refs = refs[:4], refs[4:]
+    skip = len(plan.lower) if plan.joined else 0
     kept, left = refs[:2]
     weights, slots = refs[2:5], (refs[5:12], refs[12:19])
     side_masks(left)
@@ -298,7 +303,8 @@
         if r == ROWS:
             return (above, x, 0, HALF) if x < len(plan.to_above) else (diag, 0, 0, HALF)
         if r < 0:
-            return (below, x - plan.low, LOW, HALF) if x < c else (diag, 0, LOW, HALF)
+            before = len(plan.to_above) if plan.joined else 0
+            return (below, before + x - plan.low, LOW, HALF) if x < c else (diag, 0, LOW, HALF)
         if x == c:
             return right, r, 0, TP
         if (x, r) in plan.first_a:
@@ -334,7 +340,7 @@
         if w in plan.lower:
             to_below[plan.lower.index(w)] = value[:HALF]
         if w in plan.upper:
-            to_above[plan.upper.index(w)] = value[LOW:]
+            to_above[skip + plan.upper.index(w), : T - LOW] = value[LOW:]
         if w == (plan.back_right[0] if plan.up else plan.back_right[-1]):
             to_diag[0] = value[LOW:] if plan.up else value[:HALF]
 
@@ -396,8 +402,11 @@
 
 
 def place_kernel(plan, which, d, *refs):
-    raw_c, raw_d, lefts, aboves, belows, corner = refs[:6]
-    out, fin, left, sem_out = refs[6 + which :]
+    (raw_c, raw_d, lefts, aboves), refs = refs[:4], refs[4:]
+    (belows, refs) = (aboves, refs) if plan.joined else (refs[0], refs[1:])
+    corner, refs = refs[0], refs[1 + which :]
+    out, fin, left, sem_out = refs
+    skip = len(plan.lower) if plan.joined else 0
     c = plan.c
     side_masks(left)
     where = {}
@@ -410,7 +419,7 @@
     for k, (x, _) in enumerate(plan.lower):
         where[x, -1] = (aboves, k, 0)
     for k, (x, _) in enumerate(plan.upper):
-        where[x, ROWS - 1] = (belows, k, LOW)
+        where[x, ROWS - 1] = (belows, skip + k, LOW)
     where[(-1, ROWS - 1) if plan.up else (-1, -1)] = (corner, 0, LOW if plan.up else 0)
     me = lax.axis_index("sub")
     start = (1 - me if which else me) * (c * ROWS)
@@ -465,7 +474,7 @@
 def shards(tokens, land_bits, ocean_list, w_qkv, w_out):
     window_count, _, d = tokens.shape
     mine = window_count // lax.axis_size("sub")
-    plan = Plan(mine // ROWS)
+    plan = Plan(mine // ROWS, lax.axis_size("lat"))
     turned = jnp.swapaxes(w_qkv, 2, 3)
     other_qkv, other_out = ring((turned, w_out), ("sub",), (1,))
     per_window = 12_000_000_000
@@ -473,15 +482,11 @@
     def shape(*s):
         return jax.ShapeDtypeStruct(s, bf16)
 
-    def like(a):
-        return jax.ShapeDtypeStruct(a.shape, a.dtype)
-
-    own = call(
-        functools.partial(bring_kernel, plan), [ANY] * 5,
-        [shape(mine, T, d), like(land_bits), like(ocean_list), like(turned), like(w_out)],
-        [pltpu.SemaphoreType.DMA((5,))], {}, 1_000_000, BRING, VMEM,
-    )(tokens, land_bits, ocean_list, turned, w_out)
-    weights = (own[3], own[4], other_qkv, other_out)
+    brought = call(
+        functools.partial(bring_kernel, plan), [HBM] + [VMEM] * 4, [shape(mine, T, d)],
+        [pltpu.SemaphoreType.DMA], {}, 1_000_000, BRING, VMEM,
+    )(tokens, land_bits, ocean_list, turned, w_out)[0]
+    weights = (turned, w_out, other_qkv, other_out)
     slot = [
         pltpu.VMEM((2 * TP, d), bf16), pltpu.VMEM((2 * TP, 2 * d), bf16), pltpu.VMEM((2, d, TP), bf16),
         pltpu.VMEM((2, d, TP), bf16), pltpu.VMEM((2 * TP, d), bf16), pltpu.VMEM((2, TP, 128), bf16),
@@ -494,15 +499,15 @@
         return call(
             functools.partial(first_kernel, plan, which), [VMEM] * 7, outs,
             [pltpu.VMEM((window_count, KP), f32)] + work, {}, n * per_window, LIMIT, VMEM,
-        )(*own[:3], *weights)
-
-    halves = [shape(n, SENT, d) for n in (len(plan.to_above), max(len(plan.to_below), 1), 1)]
-    first_a, left, above, below, diag = first_call(
-        0, [shape(len(plan.first_a), REC, d), shape(ROWS, REC, d)] + halves
-    )
+        )(brought, land_bits, ocean_list, *weights)
+
+    counts = (len(plan.to_above), max(len(plan.to_below), 1))
+    halves = [shape(n, SENT, d) for n in ((sum(counts),) if plan.joined else counts) + (1,)]
+    first_a, left, *bands, diag = first_call(0, [shape(len(plan.first_a), REC, d), shape(ROWS, REC, d)] + halves)
     right = beside(left, 0, -1)
-    from_below = ring(above, ("lat",), (-1,))
-    from_above = ring(below, ("lat",), (1,)) if plan.up else below
+    bands[0] = ring(bands[0], ("lat",), (-1,))
+    if plan.up and not plan.joined:
+        bands[1] = ring(bands[1], ("lat",), (1,))
     from_diag = beside(diag, 1 if plan.up else -1, -1)
     firsts = (first_a,)
     if plan.first_b:
@@ -516,32 +521,34 @@
         )(*ins)
 
     rim = len(plan.some) + len(plan.lower) + len(plan.upper)
-    raw_c, to_right, to_below, to_above, to_diag = second_call(
+    counts = (len(plan.lower), max(len(plan.upper), 1))
+    backs = [shape(sum(counts), HALF, d)] if plan.joined else [shape(counts[0], HALF, d), shape(counts[1], T - LOW, d)]
+    raw_c, to_right, *backs, to_diag = second_call(
         0,
-        firsts + weights + (right, from_below, from_above, from_diag),
+        firsts + weights + (right, *bands, from_diag),
         [
-            shape(rim, T, d), shape(ROWS, T, d), shape(len(plan.lower), HALF, d),
-            shape(max(len(plan.upper), 1), T - LOW, d), shape(1, T - LOW if plan.up else HALF, d),
+            shape(rim, T, d), shape(ROWS, T, d), *backs, shape(1, T - LOW if plan.up else HALF, d),
         ],
     )
     lefts = beside(to_right, 0, 1)
-    aboves = ring(to_below, ("lat",), (1,))
-    belows = ring(to_above, ("lat",), (-1,)) if plan.up else to_above
+    backs[0] = ring(backs[0], ("lat",), (1,))
+    if plan.up and not plan.joined:
+        backs[1] = ring(backs[1], ("lat",), (-1,))
     corner = beside(to_diag, -1 if plan.up else 1, 1)
     other_c = ring(raw_c, ("sub",), (1,))
     raw_d = raw_c
     if plan.rest:
         raw_d = second_call(1, firsts + weights + (to_diag,), [shape(len(plan.rest), T, d)])[0]
     other_d = ring(raw_d, ("sub",), (1,)) if plan.rest else other_c
-    here = (lefts, aboves, belows, corner)
+    here = (lefts, *backs, corner)
     there = ring(here, ("sub",), (1,))
 
     def place_call(which, *ins):
         return call(
-            functools.partial(place_kernel, plan, which, d), [VMEM] * 6 + [HBM] * which,
+            functools.partial(place_kernel, plan, which, d), [VMEM] * (len(ins) - which) + [HBM] * which,
             [shape(window_count, T, d)],
             [pltpu.VMEM((mine, T, d), bf16), pltpu.VMEM((T, 128), bf16), pltpu.SemaphoreType.DMA((mine,))],
-            {6: 0} if which else {}, 100_000_000, LIMIT, HBM,
+            {len(ins) - 1: 0} if which else {}, 100_000_000, LIMIT, HBM,
         )(*ins)[0]
 
     out = place_call(0, raw_c, raw_d, *here)

time: 75.2 us -> 71.1 us (0.945)
  starting transfers between devices: 14.6 us -> 11.4 us
  waiting for transfers between devices: 13.3 us -> 16.1 us
  Pallas kernels: 41.5 us -> 39.5 us
  local copies, waits for them, and re-layouts: 5.15 us -> 3.54 us
    ppermute x12 -> x9, starting transfers between devices: 7.05 us -> 4.11 us  [ring(): return lax.ppermute(value, tuple(axes), pairs)]
    ppermute x12 -> x9, waiting for transfers between devices: 7.83 us -> 10.7 us  [ring(): return lax.ppermute(value, tuple(axes), pairs)]
    pallas_call x3, Pallas kernels: 7.2 us -> 5.01 us  [the longest x2 3.31 us: place_call(): call(functools.partial(place_kernel, plan, which, d), [VMEM] * (len(ins)...]
    unnamed x14 -> x8, local copies, waits for them, and re-layouts: 5.15 us -> 3.54 us
  transfers between devices with their start and end apart: 16 -> 13, of which waited for: 5 -> 3; matrix products, arithmetic and copies ran while one was open for 0% -> 0% of each run, Pallas kernels for 31% -> 30%
where the time goes in v2:
time: 71.1 us; the launch traced here: 70.8 us
  Pallas kernels  39.5 us (56%)
  waiting for transfers between devices  16.1 us (23%)
  starting transfers between devices  11.4 us (16%)
  local copies, waits for them, and re-layouts  3.54 us (5%)
    pallas_call x2, Pallas kernels, first_call(): call(functools.partial(first_kernel, plan, which), [VMEM] * 7, outs, [plt...  18 us
    pallas_call x2, Pallas kernels, second_call(): call(functools.partial(second_kernel, plan, which, d), [VMEM] * len(ins),...  16.4 us
    ppermute x9, waiting for transfers between devices, ring(): return lax.ppermute(value, tuple(axes), pairs)  10.7 us
    ppermute x4, starting transfers between devices, beside(): lax.ppermute(value, axes, list(zip(line.ravel().tolist(), moved.ravel().t...  7.28 us
    ppermute x4, waiting for transfers between devices, beside(): lax.ppermute(value, axes, list(zip(line.ravel().tolist(), moved.ravel().t...  5.39 us
    ppermute x9, starting transfers between devices, ring(): return lax.ppermute(value, tuple(axes), pairs)  4.11 us
    unnamed x8, local copies, waits for them, and re-layouts  3.54 us
    pallas_call x2, Pallas kernels, place_call(): call(functools.partial(place_kernel, plan, which, d), [VMEM] * (len(ins)...  3.31 us
  transfers between devices with their start and end apart: 13, of which 3 were waited for; matrix products, arithmetic and copies ran while one was open for 0% of the time, Pallas kernels for 30%

profile of v2, /device:TPU:0, one launch (start us, length us, event | category | flops | bytes accessed | tf_op | source)
XLA Modules:
  0.0 70.8 jit_solution(8542992707308916320)
XLA Ops:
  0.0 0.5 collective-permute-start
  0.5 1.2 %copy-done = bf16[2,3,384,192]{2,3,1,0:T(8,128)(2,1)S(1)} copy-done((bf16[2,3,384,192]{2,3,1,0:T(8,128)(2,1)S(1)}, bf16[2,3,384,192]{2,3,1,0:T(8,128)(2,1)}, u32[]{:S(2)}) %copy-start) | copy-done | bytes 884760
  1.7 1.0 %copy-done.1 = bf16[2,192,384]{2,1,0:T(8,128)(2,1)S(1)} copy-done((bf16[2,192,384]{2,1,0:T(8,128)(2,1)S(1)}, bf16[2,192,384]{2,1,0:T(8,128)(2,1)}, u32[]{:S(2)}) %copy-start.1) | copy-done | bytes 294936
  2.6 0.8 %copy-done.2 = s32[32,200]{1,0:T(8,128)S(1)} copy-done((s32[32,200]{1,0:T(8,128)S(1)}, s32[32,200]{1,0:T(8,128)}, u32[]{:S(2)}) %copy-start.2) | copy-done | bytes 25624
  3.4 0.7 copy-done.3
  4.1 1.7 %shard_map.55.refs_0_ = bf16[16,200,384]{2,1,0:T(8,128)(2,1)S(1)} custom-call(bf16[32,200,384]{2,1,0:T(8,128)(2,1)} %tokens.1, s32[32,200]{1,0:T(8,128)S(1)} %copy-done.2, s32[1,128]{1,0:T(1,128)S(1)} %copy-done.3, bf16[2,3,192,384]{3,2,1,0:T(8,128)(2,1)S(1)} %bitcast.2, bf16[2,192,384]{2,1,0:T(8,128)(2,1)S(1)} %copy-done.1), custom_call_target="tpu_custom_call" | custom-call | flops 1000000 | bytes 4915200 | tf_op jit(solution)/shard_map/pallas_call | solution.py:485
  5.8 9.0 %shard_map.56 = (bf16[8,224,384]{2,1,0:T(8,128)(2,1)S(1)}, bf16[4,224,384]{2,1,0:T(8,128)(2,1)S(1)}, bf16[5,128,384]{2,1,0:T(8,128)(2,1)S(1)}, bf16[1,128,384]{2,1,0:T(8,128)(2,1)S(1)}) custom-call(bf16[16,200,384]{2,1,0:T(8,128)(2,1)S(1)} %shard_map.55.refs_0_, s32[32,200]{1,0:T(8,128)S(1)} %copy-done.2, s32[1,128]{1,0:T(1,128)S(1)} %copy-done.3, ...), custom_call_target="tpu_custom_call" | custom-call | flops 96000000000 | bytes 5308416 | tf_op jit(solution)/shard_map/pallas_call | solution.py:499
  14.8 5.7 %collective-permute-start.4 = (bf16[1,128,384]{2,1,0:T(8,128)(2,1)S(1)}, bf16[1,128,384]{2,1,0:T(8,128)(2,1)S(1)}, u32[]{:S(2)}, u32[]{:S(2)}) collective-permute-start(bf16[1,128,384]{2,1,0:T(8,128)(2,1)S(1)} %get-tuple-element.16), channel_id=1, source_target_pairs={{0,15},{1,2},{4,3},{5,6},{8,7},{9,10},{12,11},{13,14},{2,13},{3,0}... | collective-permute-start | bytes 294920 | tf_op jit(solution)/shard_map/ppermute | solution.py:461
  20.5 0.5 collective-permute-start.3
  21.0 0.4 collective-permute-start.2
  21.4 9.0 %shard_map.57.refs_1_ = bf16[8,224,384]{2,1,0:T(8,128)(2,1)S(1)} custom-call(bf16[16,200,384]{2,1,0:T(8,128)(2,1)S(1)} %shard_map.55.refs_0_, s32[32,200]{1,0:T(8,128)S(1)} %copy-done.2, s32[1,128]{1,0:T(1,128)S(1)} %copy-done.3, bf16[2,3,192,384]{3,2,1,0:T(8,128)(2,1)S(1)} %bitcast.4, bf16[2,192,384]{2,1,0:T(8,128)(2,1)S(1)} %copy-done.1, ...), custom_call_target="tpu_custom_call" | custom-call | flops 96000000000 | bytes 2752512 | tf_op jit(solution)/shard_map/pallas_call | solution.py:499
  30.4 1.5 %collective-permute-done.3.refs_7_ = bf16[5,128,384]{2,1,0:T(8,128)(2,1)S(1)} collective-permute-done((bf16[5,128,384]{2,1,0:T(8,128)(2,1)S(1)}, bf16[5,128,384]{2,1,0:T(8,128)(2,1)S(1)}, u32[]{:S(2)}, u32[]{:S(2)}) %collective-permute-start.3) | collective-permute-done | bytes 491552 | tf_op jit(solution)/shard_map/ppermute | solution.py:450
  32.0 7.4 %shard_map.58 = (bf16[8,200,384]{2,1,0:T(8,128)(2,1)S(1)}, bf16[4,200,384]{2,1,0:T(8,128)(2,1)S(1)}, bf16[4,112,384]{2,1,0:T(8,128)(2,1)S(1)}, bf16[1,104,384]{2,1,0:T(8,128)(2,1)S(1)}) custom-call(bf16[8,224,384]{2,1,0:T(8,128)(2,1)S(1)} %get-tuple-element.13.refs_0_, bf16[8,224,384]{2,1,0:T(8,128)(2,1)S(1)} %shard_map.57.refs_1_, ...), custom_call_target="tpu_custom_call" | custom-call | flops 96000000000 | bytes 4534272 | tf_op jit(solution)/shard_map/pallas_call | solution.py:518
  39.4 0.1 collective-permute-start.7
  39.4 1.7 %collective-permute-start.5 = (bf16[8,200,384]{2,1,0:T(8,128)(2,1)S(1)}, bf16[8,200,384]{2,1,0:T(8,128)(2,1)S(1)}, u32[]{:S(2)}, u32[]{:S(2)}) collective-permute-start(bf16[8,200,384]{2,1,0:T(8,128)(2,1)S(1)} %get-tuple-element.17.refs_0_), channel_id=1, source_target_pairs={{0,1},{1,0},{2,3},{3,2},{4,5},{5,4},{6,7},{7,6},{8,9},{9,8},{10,11... | collective-permute-start | bytes 3686408 | tf_op jit(solution)/shard_map/ppermute | solution.py:450
  41.1 9.0 %shard_map.59.refs_1_ = bf16[8,200,384]{2,1,0:T(8,128)(2,1)S(1)} custom-call(bf16[8,224,384]{2,1,0:T(8,128)(2,1)S(1)} %get-tuple-element.13.refs_0_, bf16[8,224,384]{2,1,0:T(8,128)(2,1)S(1)} %shard_map.57.refs_1_, bf16[2,3,192,384]{3,2,1,0:T(8,128)(2,1)S(1)} %bitcast.6, bf16[2,192,384]{2,1,0:T(8,128)(2,1)S(1)} %copy-done.1, ...), custom_call_target="tpu_custom_call" | custom-call | flops 96000000000 | bytes 2457600 | tf_op jit(solution)/shard_map/pallas_call | solution.py:518
  50.2 0.1 collective-permute-start.6
  50.3 1.1 %collective-permute-start.9 = (bf16[4,112,384]{2,1,0:T(8,128)(2,1)S(1)}, bf16[4,112,384]{2,1,0:T(8,128)(2,1)S(1)}, u32[]{:S(2)}, u32[]{:S(2)}) collective-permute-start(bf16[4,112,384]{2,1,0:T(8,128)(2,1)S(1)} %get-tuple-element.20), channel_id=1, source_target_pairs={{0,2},{2,0},{1,3},{3,1},{4,6},{6,4},{5,7},{7,5},{8,10},{10,8},{9,1... | collective-permute-start | bytes 1032200 | tf_op jit(solution)/shard_map/ppermute | solution.py:450
  51.4 0.2 collective-permute-start.8
  51.5 9.2 %collective-permute-done.9.refs_3_ = bf16[4,112,384]{2,1,0:T(8,128)(2,1)S(1)} collective-permute-done((bf16[4,112,384]{2,1,0:T(8,128)(2,1)S(1)}, bf16[4,112,384]{2,1,0:T(8,128)(2,1)S(1)}, u32[]{:S(2)}, u32[]{:S(2)}) %collective-permute-start.9) | collective-permute-done | bytes 344096 | tf_op jit(solution)/shard_map/ppermute | solution.py:450
  60.7 1.2 %collective-permute-start.11 = (bf16[1,104,384]{2,1,0:T(8,128)(2,1)S(1)}, bf16[1,104,384]{2,1,0:T(8,128)(2,1)S(1)}, u32[]{:S(2)}, u32[]{:S(2)}) collective-permute-start(bf16[1,104,384]{2,1,0:T(8,128)(2,1)S(1)} %get-tuple-element.18.refs_6_), channel_id=1, source_target_pairs={{0,3},{1,6},{4,7},{5,10},{8,11},{9,14},{12,15},{13,2},{2,1},{3,4},... | collective-permute-start | bytes 239624 | tf_op jit(solution)/shard_map/ppermute | solution.py:461
  61.9 5.4 %collective-permute-done.11.refs_4_ = bf16[1,104,384]{2,1,0:T(8,128)(2,1)S(1)} collective-permute-done((bf16[1,104,384]{2,1,0:T(8,128)(2,1)S(1)}, bf16[1,104,384]{2,1,0:T(8,128)(2,1)S(1)}, u32[]{:S(2)}, u32[]{:S(2)}) %collective-permute-start.11) | collective-permute-done | bytes 79904 | tf_op jit(solution)/shard_map/ppermute | solution.py:461
  67.3 1.7 %shard_map.60.refs_5_ = bf16[32,200,384]{2,1,0:T(8,128)(2,1)} custom-call(bf16[8,200,384]{2,1,0:T(8,128)(2,1)S(1)} %get-tuple-element.17.refs_0_, bf16[8,200,384]{2,1,0:T(8,128)(2,1)S(1)} %shard_map.59.refs_1_, bf16[4,200,384]{2,1,0:T(8,128)(2,1)S(1)} %collective-permute-done.7.refs_2_, bf16[4,112,384]{2,1,0:T(8,128)(2,1)S(1)} %collective-permute-done.9.refs_3_, ...), custom_call_target="tpu_custom_call" | custom-call | flops 100000000 | bytes 9830400 | tf_op jit(solution)/shard_map/pallas_call | solution.py:547
  69.0 1.7 %shard_map.61 = bf16[32,200,384]{2,1,0:T(8,128)(2,1)} custom-call(bf16[8,200,384]{2,1,0:T(8,128)(2,1)S(1)} %collective-permute-done.5.refs_0_, bf16[8,200,384]{2,1,0:T(8,128)(2,1)S(1)} %collective-permute-done.6.refs_1_, bf16[4,200,384]{2,1,0:T(8,128)(2,1)S(1)} %collective-permute-done.8.refs_2_, ...), custom_call_target="tpu_custom_call", output_to_operand_aliasing={{}: (5, {})} | custom-call | flops 100000000 | bytes 9830400 | tf_op jit(solution)/shard_map/pallas_call | solution.py:547
  (17 shorter events, 0.1 us)
Async XLA Ops:
  0.0 5.8 %collective-permute-start = (bf16[2,3,192,384]{3,2,1,0:T(8,128)(2,1)}, bf16[2,3,192,384]{3,2,1,0:T(8,128)(2,1)S(1)}, u32[]{:S(2)}, u32[]{:S(2)}) collective-permute-start(bf16[2,3,192,384]{3,2,1,0:T(8,128)(2,1)} %bitcast.1), channel_id=1, source_target_pairs={{0,1},{1,0},{2,3},{3,2},{4,5},{5,4},{6,7},{7,6},{8,9},{9,8},{10,11... | collective-permute-start | bytes 2654216 | tf_op jit(solution)/shard_map/ppermute | solution.py:450
  0.5 5.3 %collective-permute-start.1 = (bf16[2,192,384]{2,1,0:T(8,128)(2,1)}, bf16[2,192,384]{2,1,0:T(8,128)(2,1)S(1)}, u32[]{:S(2)}, u32[]{:S(2)}) collective-permute-start(bf16[2,192,384]{2,1,0:T(8,128)(2,1)} %refs_3_.3), channel_id=1, source_target_pairs={{0,1},{1,0},{2,3},{3,2},{4,5},{5,4},{6,7},{7,6},{8,9},{9,8},{10,11... | collective-permute-start | bytes 884744 | tf_op jit(solution)/shard_map/ppermute | solution.py:450
  0.5 1.2 %copy-start = (bf16[2,3,384,192]{2,3,1,0:T(8,128)(2,1)S(1)}, bf16[2,3,384,192]{2,3,1,0:T(8,128)(2,1)}, u32[]{:S(2)}) copy-start(bf16[2,3,384,192]{2,3,1,0:T(8,128)(2,1)} %param.8) | copy-start | bytes 2654212
  1.7 1.0 %copy-start.1 = (bf16[2,192,384]{2,1,0:T(8,128)(2,1)S(1)}, bf16[2,192,384]{2,1,0:T(8,128)(2,1)}, u32[]{:S(2)}) copy-start(bf16[2,192,384]{2,1,0:T(8,128)(2,1)} %refs_3_.3) | copy-start | bytes 884740
  2.6 0.8 %copy-start.2 = (s32[32,200]{1,0:T(8,128)S(1)}, s32[32,200]{1,0:T(8,128)}, u32[]{:S(2)}) copy-start(s32[32,200]{1,0:T(8,128)} %refs_1_.3) | copy-start | bytes 76804
  3.4 0.7 copy-start.3
  14.8 15.6 %collective-permute-start.4 = (bf16[1,128,384]{2,1,0:T(8,128)(2,1)S(1)}, bf16[1,128,384]{2,1,0:T(8,128)(2,1)S(1)}, u32[]{:S(2)}, u32[]{:S(2)}) collective-permute-start(bf16[1,128,384]{2,1,0:T(8,128)(2,1)S(1)} %get-tuple-element.16), channel_id=1, source_target_pairs={{0,15},{1,2},{4,3},{5,6},{8,7},{9,10},{12,11},{13,14},{2,13},{3,0}... | collective-permute-start | bytes 294920 | tf_op jit(solution)/shard_map/ppermute | solution.py:461
  20.5 11.5 %collective-permute-start.3 = (bf16[5,128,384]{2,1,0:T(8,128)(2,1)S(1)}, bf16[5,128,384]{2,1,0:T(8,128)(2,1)S(1)}, u32[]{:S(2)}, u32[]{:S(2)}) collective-permute-start(bf16[5,128,384]{2,1,0:T(8,128)(2,1)S(1)} %get-tuple-element.15), channel_id=1, source_target_pairs={{0,2},{2,0},{1,3},{3,1},{4,6},{6,4},{5,7},{7,5},{8,10},{10,8},{9,1... | collective-permute-start | bytes 1474568 | tf_op jit(solution)/shard_map/ppermute | solution.py:450
  21.0 10.9 %collective-permute-start.2 = (bf16[4,224,384]{2,1,0:T(8,128)(2,1)S(1)}, bf16[4,224,384]{2,1,0:T(8,128)(2,1)S(1)}, u32[]{:S(2)}, u32[]{:S(2)}) collective-permute-start(bf16[4,224,384]{2,1,0:T(8,128)(2,1)S(1)} %get-tuple-element.14), channel_id=1, source_target_pairs={{0,13},{1,0},{4,1},{5,4},{8,5},{9,8},{12,9},{13,12},{2,15},{3,2},{... | collective-permute-start | bytes 2064392 | tf_op jit(solution)/shard_map/ppermute | solution.py:461
  39.4 12.0 %collective-permute-start.7 = (bf16[4,200,384]{2,1,0:T(8,128)(2,1)S(1)}, bf16[4,200,384]{2,1,0:T(8,128)(2,1)S(1)}, u32[]{:S(2)}, u32[]{:S(2)}) collective-permute-start(bf16[4,200,384]{2,1,0:T(8,128)(2,1)S(1)} %get-tuple-element.19), channel_id=1, source_target_pairs={{0,1},{1,4},{4,5},{5,8},{8,9},{9,12},{12,13},{13,0},{2,3},{3,6},{6... | collective-permute-start | bytes 1843208 | tf_op jit(solution)/shard_map/ppermute | solution.py:461
  39.4 29.5 %collective-permute-start.5 = (bf16[8,200,384]{2,1,0:T(8,128)(2,1)S(1)}, bf16[8,200,384]{2,1,0:T(8,128)(2,1)S(1)}, u32[]{:S(2)}, u32[]{:S(2)}) collective-permute-start(bf16[8,200,384]{2,1,0:T(8,128)(2,1)S(1)} %get-tuple-element.17.refs_0_), channel_id=1, source_target_pairs={{0,1},{1,0},{2,3},{3,2},{4,5},{5,4},{6,7},{7,6},{8,9},{9,8},{10,11... | collective-permute-start | bytes 3686408 | tf_op jit(solution)/shard_map/ppermute | solution.py:450
  50.2 18.8 %collective-permute-start.6 = (bf16[8,200,384]{2,1,0:T(8,128)(2,1)S(1)}, bf16[8,200,384]{2,1,0:T(8,128)(2,1)S(1)}, u32[]{:S(2)}, u32[]{:S(2)}) collective-permute-start(bf16[8,200,384]{2,1,0:T(8,128)(2,1)S(1)} %shard_map.59.refs_1_), channel_id=1, source_target_pairs={{0,1},{1,0},{2,3},{3,2},{4,5},{5,4},{6,7},{7,6},{8,9},{9,8},{10,11... | collective-permute-start | bytes 3686408 | tf_op jit(solution)/shard_map/ppermute | solution.py:450
  50.3 10.5 %collective-permute-start.9 = (bf16[4,112,384]{2,1,0:T(8,128)(2,1)S(1)}, bf16[4,112,384]{2,1,0:T(8,128)(2,1)S(1)}, u32[]{:S(2)}, u32[]{:S(2)}) collective-permute-start(bf16[4,112,384]{2,1,0:T(8,128)(2,1)S(1)} %get-tuple-element.20), channel_id=1, source_target_pairs={{0,2},{2,0},{1,3},{3,1},{4,6},{6,4},{5,7},{7,5},{8,10},{10,8},{9,1... | collective-permute-start | bytes 1032200 | tf_op jit(solution)/shard_map/ppermute | solution.py:450
  51.4 17.6 %collective-permute-start.8 = (bf16[4,200,384]{2,1,0:T(8,128)(2,1)S(1)}, bf16[4,200,384]{2,1,0:T(8,128)(2,1)S(1)}, u32[]{:S(2)}, u32[]{:S(2)}) collective-permute-start(bf16[4,200,384]{2,1,0:T(8,128)(2,1)S(1)} %collective-permute-done.7.refs_2_), channel_id=1, source_target_pairs={{0,1},{1,0},{2,3},{3,2},{4,5},{5,4},{6,7},{7,6},{8,9},{9,8},{10,11... | collective-permute-start | bytes 1843208 | tf_op jit(solution)/shard_map/ppermute | solution.py:450
  60.7 8.2 %collective-permute-start.10 = (bf16[4,112,384]{2,1,0:T(8,128)(2,1)S(1)}, bf16[4,112,384]{2,1,0:T(8,128)(2,1)S(1)}, u32[]{:S(2)}, u32[]{:S(2)}) collective-permute-start(bf16[4,112,384]{2,1,0:T(8,128)(2,1)S(1)} %collective-permute-done.9.refs_3_), channel_id=1, source_target_pairs={{0,1},{1,0},{2,3},{3,2},{4,5},{5,4},{6,7},{7,6},{8,9},{9,8},{10,11... | collective-permute-start | bytes 1032200 | tf_op jit(solution)/shard_map/ppermute | solution.py:450
  60.7 6.5 %collective-permute-start.11 = (bf16[1,104,384]{2,1,0:T(8,128)(2,1)S(1)}, bf16[1,104,384]{2,1,0:T(8,128)(2,1)S(1)}, u32[]{:S(2)}, u32[]{:S(2)}) collective-permute-start(bf16[1,104,384]{2,1,0:T(8,128)(2,1)S(1)} %get-tuple-element.18.refs_6_), channel_id=1, source_target_pairs={{0,3},{1,6},{4,7},{5,10},{8,11},{9,14},{12,15},{13,2},{2,1},{3,4},... | collective-permute-start | bytes 239624 | tf_op jit(solution)/shard_map/ppermute | solution.py:461
  67.3 1.7 %collective-permute-start.12 = (bf16[1,104,384]{2,1,0:T(8,128)(2,1)S(1)}, bf16[1,104,384]{2,1,0:T(8,128)(2,1)S(1)}, u32[]{:S(2)}, u32[]{:S(2)}) collective-permute-start(bf16[1,104,384]{2,1,0:T(8,128)(2,1)S(1)} %collective-permute-done.11.refs_4_), channel_id=1, source_target_pairs={{0,1},{1,0},{2,3},{3,2},{4,5},{5,4},{6,7},{7,6},{8,9},{9,8},{10,11... | collective-permute-start | bytes 239624 | tf_op jit(solution)/shard_map/ppermute | solution.py:450
